TPU v7x, 32 devices: a whole 2x2x4 slice. The times are simulated.
32 devices in a mesh: req: 4 (over z), seq: 8 (over y, x, core).
Axes of the slice: x: 2, y: 2, z: 4, core: 2. Of those that a mesh axis runs over, the one named last changes fastest.
Arguments:
- tokens: bfloat16 [32, 4, 2560], P('req'), may hold values from -6 to 6
- slot_of: int32 [32], replicated, may hold values from 0 to 31, each once
- cache_len: int32 [32], P('req'), may hold values from 1 to 4096, 32768 in all
- owner_shard: int32 [32, 4], P('req'), may hold values from 0 to 7
- cache_keys: bfloat16 [32, 4096, 1024], P('req', 'seq'), may hold values from -40 to 40
- stored_values: bfloat16 [32, 4096, 1024], P('req', 'seq'), may hold values from -6 to 6
- attn_gain: float32 [2560], replicated, may hold values from 0.5 to 1.5
- w_query: bfloat16 [2560, 4096], P(None, 'seq'), may hold values from -0.125 to 0.125
- key_matrix: bfloat16 [2560, 1024], P(None, 'seq'), may hold values from -0.125 to 0.125
- value_matrix: bfloat16 [2560, 1024], P(None, 'seq'), may hold values from -0.125 to 0.125
- query_gain: float32 [128], replicated, may hold values from 0.5 to 40
- key_norm_weight: float32 [128], replicated, may hold values from 0.5 to 8
- w_out: bfloat16 [4096, 2560], P('seq'), may hold values from -0.09375 to 0.09375
- mlp_gain: float32 [2560], replicated, may hold values from 0.5 to 1.5
- w_gate: bfloat16 [2560, 9728], P(None, ('req', 'seq')), may hold values from -0.125 to 0.125
- w_up: bfloat16 [2560, 9728], P(None, ('req', 'seq')), may hold values from -0.125 to 0.125
- w_down: bfloat16 [9728, 2560], P(('req', 'seq')), may hold values from -0.0625 to 0.0625
Outputs:
- outputs: bfloat16 [32, 4, 2560], P('req')
- appended: bfloat16 [32, 8, 4, 2048], P('req', 'seq')
Inputs may be any that keep to these rules, and one draw needn't show every extreme that they name: `slot_of`: each slot appears once. `cache_len`: one slot has exactly 4096 cached positions; the lengths sum to 32768.
All inputs are finite; a program needn't handle non-finite values. No bound on the sum of `cache_len` on one device may be relied on, other than what follows from the above.
Results may differ from a plain program's by a relative error of at most 0.012.
The roundings to bfloat16 on the way count: a program that leaves them out, or rounds other values in their place, can miss the bound.
Values may be sent and summed in bfloat16 or wider, within the bound.
A program may use at most 128 MiB of HBM per device.

v0:
```python
import functools
import math

import jax
import jax.numpy as jnp
from jax import lax
from jax.experimental import pallas as pl
from jax.experimental.pallas import tpu as pltpu
from jax.sharding import PartitionSpec as P

EPSILON = 1e-06
ROPE_BASE = 1000000.0
MASKED = -1e30


def root_mean_scale(tensor, gain_vec):
    mean_square = jnp.mean(tensor * tensor, axis=-1, keepdims=True)
    return tensor * lax.rsqrt(mean_square + EPSILON) * gain_vec


def apply_rotary(tensor, positions):
    half_dim = tensor.shape[-1] // 2
    frequency = ROPE_BASE ** (-2.0 * jnp.arange(half_dim, dtype=jnp.float32) / tensor.shape[-1])
    angles = positions[..., None] * frequency
    cosine = jnp.cos(angles)
    sine_part = jnp.sin(angles)
    front_half = tensor[..., :half_dim]
    back_half = tensor[..., half_dim:]
    return jnp.concatenate(
        [front_half * cosine - back_half * sine_part, back_half * cosine + front_half * sine_part],
        axis=-1,
    )


def attention_kernel(kv_heads, query_heads, here_ref, live_ref, q_ref, k_ref, v_ref, fk_ref, fv_ref,
                     out_ref, max_ref, sum_ref):
    slot = pl.program_id(0)
    rows, head_dim = q_ref.shape[1], q_ref.shape[2]
    span = k_ref.shape[1]
    pad = fk_ref.shape[1]
    width = kv_heads * head_dim
    group = query_heads // kv_heads
    scale = 1.0 / math.sqrt(head_dim)
    own_kv = lax.rem(lax.broadcasted_iota(jnp.int32, (rows, width), 0), query_heads) // group
    lane_kv = lax.broadcasted_iota(jnp.int32, (rows, width), 1) // head_dim
    q = q_ref[0]
    wide = jnp.where(own_kv == lane_kv, jnp.concatenate([q] * kv_heads, axis=1), jnp.zeros((), q.dtype))
    nt = (((1,), (1,)), ((), ()))
    scores = lax.dot_general(wide, k_ref[0], nt, preferred_element_type=jnp.float32) * scale
    in_cache = lax.broadcasted_iota(jnp.int32, (rows, span), 1) < here_ref[slot]
    scores = jnp.where(in_cache, scores, MASKED)
    fresh = lax.dot_general(wide, fk_ref[0], nt, preferred_element_type=jnp.float32) * scale
    step_row = lax.broadcasted_iota(jnp.int32, (rows, pad), 0) // query_heads
    step_lane = lax.broadcasted_iota(jnp.int32, (rows, pad), 1)
    live = (step_lane <= step_row) & (live_ref[0, 0:1, :] > 0)
    fresh = jnp.where(live, fresh, MASKED)
    top = jnp.maximum(
        jnp.max(scores, axis=1, keepdims=True), jnp.max(fresh, axis=1, keepdims=True)
    )
    weights = jnp.where(in_cache, jnp.exp(scores - top), 0.0)
    fresh_weights = jnp.where(live, jnp.exp(fresh - top), 0.0)
    total = jnp.sum(weights, axis=1, keepdims=True) + jnp.sum(fresh_weights, axis=1, keepdims=True)
    product = jnp.dot(weights.astype(jnp.bfloat16), v_ref[0], preferred_element_type=jnp.float32)
    product = product + jnp.dot(
        fresh_weights.astype(jnp.bfloat16), fv_ref[0], preferred_element_type=jnp.float32
    )
    product = jnp.where(own_kv == lane_kv, product, 0.0)
    picked = product[:, :head_dim]
    for head in range(1, kv_heads):
        picked = picked + product[:, head * head_dim:(head + 1) * head_dim]
    out_ref[0] = picked
    max_ref[0] = jnp.broadcast_to(top, (rows, head_dim))
    sum_ref[0] = jnp.broadcast_to(total, (rows, head_dim))


def body(
    tokens,
    slot_of,
    cache_len,
    owner_shard,
    cache_keys,
    stored_values,
    attn_gain,
    w_query,
    key_matrix,
    value_matrix,
    query_gain,
    key_norm_weight,
    w_out,
    mlp_gain,
    w_gate,
    w_up,
    w_down,
):
    group_id = lax.axis_index("req")
    shard_id = lax.axis_index("seq")
    shard_count = lax.axis_size("seq")
    row_count = cache_len.shape[0]
    span_len = cache_keys.shape[1]
    step_count, model_width = tokens.shape[1:]
    head_dim = query_gain.shape[0]
    kv_heads = cache_keys.shape[2] // head_dim
    query_heads = w_query.shape[1] * shard_count // head_dim
    heads_here = query_heads // shard_count
    all_rows = row_count * step_count
    arrived = lax.all_gather(tokens, "req", axis=0, tiled=True)
    slot_ids = group_id * row_count + jnp.arange(row_count, dtype=jnp.int32)
    selector = (slot_of[None, :] == slot_ids[:, None]).astype(jnp.bfloat16)
    inputs = jnp.einsum("ji,isd->jsd", selector, arrived, preferred_element_type=jnp.float32)
    current = inputs.reshape(all_rows, model_width)
    normed = root_mean_scale(current, attn_gain).astype(jnp.bfloat16)
    parts = [
        jnp.dot(normed, matrix, preferred_element_type=jnp.float32).astype(jnp.bfloat16)
        for matrix in (w_query, key_matrix, value_matrix)
    ]
    cut = [parts[0].shape[1], parts[0].shape[1] + parts[1].shape[1]]
    gathered = lax.all_gather(jnp.concatenate(parts, axis=1), "seq", axis=0)
    gathered = jnp.transpose(gathered, (1, 0, 2))
    query_raw = gathered[:, :, :cut[0]].reshape(row_count, step_count, query_heads, head_dim)
    key_raw = gathered[:, :, cut[0]:cut[1]].reshape(row_count, step_count, kv_heads, head_dim)
    incoming_values = gathered[:, :, cut[1]:].reshape(row_count, step_count, kv_heads * head_dim)
    position = (cache_len[:, None] + jnp.arange(step_count, dtype=jnp.int32)).astype(jnp.float32)
    queries = apply_rotary(
        root_mean_scale(query_raw.astype(jnp.float32), query_gain), position[..., None]
    ).astype(jnp.bfloat16)
    incoming_keys = apply_rotary(
        root_mean_scale(key_raw.astype(jnp.float32), key_norm_weight), position[..., None]
    ).astype(jnp.bfloat16).reshape(row_count, step_count, kv_heads * head_dim)
    owned_here = owner_shard == shard_id
    pad = 128
    widen = ((0, 0), (0, pad - step_count), (0, 0))
    live = jnp.pad(owned_here.astype(jnp.int32), ((0, 0), (0, pad - step_count)))
    live = jnp.broadcast_to(live[:, None, :], (row_count, 8, pad))
    here = cache_len - shard_id * span_len
    packed_rows = step_count * query_heads
    wide_dim = kv_heads * head_dim
    slot_block = lambda *shape: pl.BlockSpec((1,) + shape, lambda i, *_: (i,) + (0,) * len(shape))
    out_type = jax.ShapeDtypeStruct((row_count, packed_rows, head_dim), jnp.float32)
    block_out, block_max, block_sum = pl.pallas_call(
        functools.partial(attention_kernel, kv_heads, query_heads),
        out_shape=(out_type,) * 3,
        grid_spec=pltpu.PrefetchScalarGridSpec(
            num_scalar_prefetch=1,
            grid=(row_count,),
            in_specs=[
                slot_block(8, pad),
                slot_block(packed_rows, head_dim),
                slot_block(span_len, wide_dim),
                slot_block(span_len, wide_dim),
                slot_block(pad, wide_dim),
                slot_block(pad, wide_dim),
            ],
            out_specs=[slot_block(packed_rows, head_dim)] * 3,
        ),
    )(
        here,
        live,
        queries.reshape(row_count, packed_rows, head_dim),
        cache_keys,
        stored_values,
        jnp.pad(incoming_keys, widen),
        jnp.pad(incoming_values, widen),
    )
    split = lambda a: a.reshape(all_rows, shard_count, heads_here, -1)
    stats = jnp.concatenate([split(block_max)[..., :1], split(block_sum)[..., :1]], axis=-1)
    payload = jnp.concatenate(
        [
            split(block_out).reshape(all_rows, shard_count, -1),
            stats.reshape(all_rows, shard_count, -1),
        ],
        axis=-1,
    )
    traded = lax.all_to_all(payload, "seq", split_axis=1, concat_axis=0, tiled=False)
    wide_out = heads_here * head_dim
    outs = traded[..., :wide_out].reshape(shard_count, all_rows, heads_here, head_dim)
    stats = traded[..., wide_out:].reshape(shard_count, all_rows, heads_here, 2)
    top = jnp.max(stats[..., 0], axis=0)
    factor = jnp.exp(stats[..., 0] - top)
    numer = jnp.sum(factor[..., None] * outs, axis=0)
    denom = jnp.sum(factor * stats[..., 1], axis=0)
    attended = (numer / denom[..., None]).astype(jnp.bfloat16).reshape(all_rows, wide_out)
    projected = lax.psum_scatter(
        jnp.dot(attended, w_out, preferred_element_type=jnp.float32),
        "seq",
        scatter_dimension=0,
        tiled=True,
    )
    rows_here = all_rows // shard_count
    residual = projected + lax.dynamic_slice_in_dim(current, shard_id * rows_here, rows_here, 0)
    mlp_in = root_mean_scale(residual, mlp_gain).astype(jnp.bfloat16)
    piece = lax.all_gather(mlp_in, ("req", "seq"), axis=0, tiled=True)
    gate_part = jnp.dot(piece, w_gate, preferred_element_type=jnp.float32)
    up_part = jnp.dot(piece, w_up, preferred_element_type=jnp.float32)
    hidden = (jax.nn.silu(gate_part) * up_part).astype(jnp.bfloat16)
    down = lax.psum_scatter(
        jnp.dot(hidden, w_down, preferred_element_type=jnp.float32),
        ("req", "seq"),
        scatter_dimension=0,
        tiled=True,
    )
    finished = (residual + down).astype(jnp.bfloat16)
    outputs = lax.all_gather(finished, "seq", axis=0, tiled=True)
    outputs = outputs.reshape(row_count, step_count, model_width)
    stacked_incoming = jnp.concatenate([incoming_keys, incoming_values], axis=-1)
    appended = jnp.where(owned_here[..., None], stacked_incoming, jnp.zeros((), jnp.bfloat16))
    return (outputs, appended[:, None])


def solution(mesh):
    in_specs = (
        P("req", None, None),
        P(),
        P("req"),
        P("req", None),
        P("req", "seq", None),
        P("req", "seq", None),
        P(),
        P(None, "seq"),
        P(None, "seq"),
        P(None, "seq"),
        P(),
        P(),
        P("seq", None),
        P(),
        P(None, ("req", "seq")),
        P(None, ("req", "seq")),
        P(("req", "seq"), None),
    )
    out_specs = (P("req", None, None), P("req", "seq", None, None))
    return jax.shard_map(body, mesh=mesh, in_specs=in_specs, out_specs=out_specs, check_vma=False)
```

profile of v0, /device:TPU:0, one launch (start us, length us, event | category | flops | bytes accessed | tf_op | source)
XLA Modules:
  0.0 346.6 jit_solution(7292687982667425473)
XLA Ops:
  7.2 0.0 copy-start
  7.2 0.0 all-reduce.8.cloned.1.call-start
  7.3 1.1 copy.56
  8.4 19.6 %all_gather.15 = bf16[32,4,2560]{2,0,1:T(8,128)(2,1)S(1)} all-gather(bf16[8,4,2560]{2,0,1:T(8,128)(2,1)S(1)} %copy.56), channel_id=1, replica_groups=mesh['req'=4,'seq'=8] {'req'}, dimensions={0}, use_global_device_ids=true | all-gather | bytes 819200 | tf_op jit(solution)/shard_map/all_gather | solution.py:106
  28.0 1.0 multiply_reduce_fusion.1
  29.0 0.1 copy.58
  29.1 0.1 rsqrt.39
  29.2 0.2 copy.57
  29.4 0.1 reshape.178
  29.5 0.1 multiply_convert_fusion
  29.6 1.3 convolution_convert_fusion.1
  31.0 1.3 convolution_convert_fusion.2
  32.3 0.0 copy-start.5
  32.3 2.3 convolution_convert_fusion
  34.6 9.6 %all-gather = bf16[256,768]{1,0:T(8,128)(2,1)S(1)} all-gather(bf16[32,768]{1,0:T(8,128)(2,1)S(1)} %pad_maximum_fusion.2), channel_id=2, replica_groups=mesh['req'=4,'seq'=8] {'seq'}, dimensions={0}, use_global_device_ids=true | all-gather | bytes 442368 | tf_op jit(solution)/shard_map/all_gather | solution.py:117
  44.2 0.2 copy.68
  44.5 0.1 multiply_reduce_fusion.2
  44.6 0.8 slice_convert_fusion
  45.5 0.1 add_convert_fusion.2
  45.5 0.5 broadcast_subtract_fusion.here_ref
  46.0 0.1 copy.55
  46.2 0.2 multiply_cosine_fusion
  46.4 0.1 multiply_multiply_fusion.1
  46.5 0.1 subtract_convert_fusion.1
  46.6 0.1 pad_maximum_fusion.1
  46.7 0.6 copy-done.2
  47.3 1.1 reshape.185
  48.4 0.2 multiply_reduce_fusion
  48.7 0.2 multiply_multiply_fusion
  48.9 0.2 subtract_convert_fusion
  49.1 1.6 pad.17.fv_ref
  50.7 1.6 pad.16.fk_ref
  52.3 0.8 pad_maximum_fusion.q_ref
  53.1 0.6 broadcast_in_dim.12.live_ref
  53.8 15.1 %shard_map.176 = (f32[8,128,128]{2,1,0:T(8,128)}, f32[8,128,128]{2,1,0:T(8,128)}, f32[8,128,128]{2,1,0:T(8,128)}) custom-call(s32[8]{0:T(128)} %broadcast_subtract_fusion.here_ref, s32[8,8,128]{2,1,0:T(8,128)} %broadcast_in_dim.12.live_ref, bf16[8,128,128]{2,1,0:T(8,128)(2,1)} %pad_maximum_fusion.q_ref, bf16[8,512,1024]{2,1,0:T(8,128)(2,1)} %k_ref.1, ...), custom_call_target="tpu_custom_call" | custom-call | tf_op jit(solution)/shard_map/pallas_call | solution.py:139
  68.9 1.9 reshape_reshape.3
  70.8 1.3 copy.62
  72.1 1.4 copy.65
  73.5 1.4 copy.66
  74.9 0.1 copy.63
  75.0 0.1 maximum_bitcast_fusion
  75.0 13.7 %all_to_all.15 = f32[1,32,8,520]{3,1,0,2:T(8,128)S(1)} all-to-all(f32[1,32,8,520]{3,1,0,2:T(8,128)S(1)} %maximum_bitcast_fusion), channel_id=1, replica_groups=mesh['req'=4,'seq'=8] {'seq'}, dimensions={2} | all-to-all | bytes 1064960 | tf_op jit(solution)/shard_map/all_to_all | solution.py:173
  88.8 2.0 copy.64
  90.8 0.8 slice.62
  91.6 2.2 fusion
  93.8 0.0 copy-start.9
  93.9 1.3 fusion.23
  95.2 0.0 all-reduce.8.cloned.1.call-update
  95.2 0.0 all-reduce.10.cloned.1.call-start
  95.3 0.6 dynamic-slice
  96.5 51.1 %all-reduce.8.cloned.1.call-done = f32[32,2560]{1,0:T(8,128)} async-done(((f32[32,2560]{1,0:T(8,128)}), f32[32,2560]{1,0:T(8,128)}) %all-reduce.8.cloned.1.call-update) | async-done | bytes 327696
  147.7 1.1 multiply_reduce_fusion.3
  148.7 0.1 fusion.11
  148.8 44.4 %all-gather.1 = bf16[32,4,2560]{2,1,0:T(4,128)(2,1)} all-gather(bf16[1,4,2560]{2,1,0:T(4,128)(2,1)S(1)} %fusion.11), channel_id=1, replica_groups=mesh['req'=4,'seq'=8] {'req','seq'}, dimensions={0}, use_global_device_ids=true | all-gather | bytes 675840 | tf_op jit(solution)/shard_map/all_gather | solution.py:191
  193.2 1.5 reshape.189
  194.7 2.0 fusion.24
  196.7 4.7 %fusion.2 = f32[128,2560]{1,0:T(8,128)} fusion(bf16[304,2560]{1,0:T(8,128)(2,1)} %param.33, bf16[128,2560]{1,0:T(8,128)(2,1)S(1)} %reshape.189, bf16[2560,304]{0,1:T(8,128)(2,1)} %param.32, f32[128,304]{0,1:T(8,128)S(1)} %fusion.24), kind=kOutput, calls=%fused_computation.4 | convolution fusion | flops 398692352 | bytes 5234688 | tf_op jit(solution)/shard_map/dot_general | solution.py:196
  201.4 0.0 all-reduce.10.cloned.1.call-update
  201.4 0.9 concatenate.43
  202.3 0.8 maximum_select_fusion
  203.1 125.9 %all-reduce.10.cloned.1.call-done = f32[128,2560]{1,0:T(8,128)} async-done(((f32[128,2560]{1,0:T(8,128)}), f32[128,2560]{1,0:T(8,128)}) %all-reduce.10.cloned.1.call-update) | async-done | bytes 1310736
  329.0 0.9 fusion.12
  329.9 9.2 %all-gather.2 = bf16[8,4,2560]{2,1,0:T(4,128)(2,1)S(1)} all-gather(bf16[1,4,2560]{2,1,0:T(4,128)(2,1)S(1)} %fusion.12), channel_id=1, replica_groups=mesh['req'=4,'seq'=8] {'seq'}, dimensions={0}, use_global_device_ids=true | all-gather | bytes 184320 | tf_op jit(solution)/shard_map/all_gather | solution.py:202
  339.1 0.7 copy.72
  (34 shorter events, 0.3 us)
Async XLA Ops:
  7.2 86.7 %copy-start = (bf16[512,2560]{1,0:T(8,128)(2,1)S(1)}, bf16[512,2560]{1,0:T(8,128)(2,1)}, u32[]{:S(2)}) copy-start(bf16[512,2560]{1,0:T(8,128)(2,1)} %param.29) | copy-start | bytes 7864324
  7.2 22.3 %copy-start.4 = (f32[2560]{0:T(1024)S(1)}, f32[2560]{0:T(1024)}, u32[]{:S(2)}) copy-start(f32[2560]{0:T(1024)} %param.23) | copy-start | bytes 30724
  7.2 140.5 %all-reduce.8.cloned.1.call-start = ((), (), s32[]{:S(2)}) async-start(), calls=%async_computation.1 | async-start | bytes 655360
  29.5 5.1 %copy-start.1 = (f32[32,2560]{1,0:T(8,128)}, f32[32,2560]{1,0:T(8,128)S(1)}, u32[]{:S(2)}) copy-start(f32[32,2560]{1,0:T(8,128)S(1)} %reshape.178) | copy-start | bytes 983044
  32.3 13.2 %copy-start.8 = (s32[8]{0:T(128)S(1)}, s32[8]{0:T(128)}, u32[]{:S(2)}) copy-start(s32[8]{0:T(128)} %param.19) | copy-start | bytes 100
  32.3 13.8 %copy-start.5 = (s32[8,4]{0,1:T(4,128)S(1)}, s32[8,4]{0,1:T(4,128)}, u32[]{:S(2)}) copy-start(s32[8,4]{0,1:T(4,128)} %param.20) | copy-start | bytes 388
  32.3 14.1 %copy-start.6 = (f32[128]{0:T(128)S(1)}, f32[128]{0:T(128)}, u32[]{:S(2)}) copy-start(f32[128]{0:T(128)} %param.28) | copy-start | bytes 1540
  44.5 4.2 %copy-start.7 = (f32[128]{0:T(128)S(1)}, f32[128]{0:T(128)}, u32[]{:S(2)}) copy-start(f32[128]{0:T(128)} %param.27) | copy-start | bytes 1540
  46.7 0.6 copy-start.2
  93.8 1.5 copy-start.9
  93.9 54.9 %copy-start.3 = (f32[2560]{0:T(1024)S(1)}, f32[2560]{0:T(1024)}, u32[]{:S(2)}) copy-start(f32[2560]{0:T(1024)} %param.30) | copy-start | bytes 30724
  95.2 233.8 %all-reduce.10.cloned.1.call-start = ((), (), s32[]{:S(2)}) async-start(), calls=%async_computation.2 | async-start | bytes 2621440
Sparse Core Ops, SparseCore 0:
  95.4 52.2 all-reduce.7
  201.5 127.4 all-reduce.9
where the time goes:
time: 348 us; the launch traced here: 347 us
  waiting for transfers between devices  177 us (51%)
  blocking collectives  96.6 us (28%)
  local copies, waits for them, and re-layouts  19.9 us (6%)
  Pallas kernels  15.1 us (4%)
  between operations  15 us (4%)
  matrix products  13.9 us (4%)
  other arithmetic  8.93 us (3%)
    unnamed x4, waiting for transfers between devices  177 us
    all_gather x1, blocking collectives, body(): piece = lax.all_gather(mlp_in, ('req', 'seq'), axis=0, tiled=True)  44.4 us
    all_gather x1, blocking collectives, body(): arrived = lax.all_gather(tokens, 'req', axis=0, tiled=True)  19.6 us
    pallas_call x1, Pallas kernels, body(): pl.pallas_call(functools.partial(attention_kernel, kv_heads, query_heads)...  15.1 us
    all_to_all x1, blocking collectives, body(): lax.all_to_all(payload, 'seq', split_axis=1, concat_axis=0, tiled=False)  13.7 us
    all_gather x1, blocking collectives, body(): gathered = lax.all_gather(jnp.concatenate(parts, axis=1), 'seq', axis=0)  9.59 us
    all_gather x1, blocking collectives, body(): outputs = lax.all_gather(finished, 'seq', axis=0, tiled=True)  9.2 us
    unnamed x27, local copies, waits for them, and re-layouts  7.29 us
  transfers between devices with their start and end apart: 2, of which 2 were waited for; matrix products, arithmetic and copies ran while one was open for 1% of the time, Pallas kernels for 0%

commit v1 on v0

--- a/solution.py
+++ b/solution.py
@@ -71,6 +71,159 @@
     out_ref[0] = picked
     max_ref[0] = jnp.broadcast_to(top, (rows, head_dim))
     sum_ref[0] = jnp.broadcast_to(total, (rows, head_dim))
+
+
+def tail_kernel(ring, plane, steps, attended_ref, current_ref, gain_ref, w_out_hbm, gate_hbm, up_hbm,
+                down_hbm, out_ref, w_out, w_gate, w_up, w_down, proj_send, proj_land, mlp_all, half_send,
+                half_land, quad_send, quad_land, ring_send, ring_land, final, weight_sem, send_sem, recv_sem):
+    group = lax.axis_index("req")
+    shard = lax.axis_index("seq")
+    chips = plane // 2
+    core, chip = lax.rem(shard, 2), shard // 2
+    other = 1 - core
+    partner = chip * 2 + other
+    order = core * chips + chip
+    mesh_type = pl.DeviceIdType.MESH
+
+    weights = [
+        pltpu.make_async_copy(src, dst, weight_sem.at[i])
+        for i, (src, dst) in enumerate(
+            ((w_out_hbm, w_out), (gate_hbm, w_gate), (up_hbm, w_up), (down_hbm, w_down))
+        )
+    ]
+    for copy in weights:
+        copy.start()
+    plane_peers = [lax.rem(shard + d, plane) for d in range(1, plane)]
+    ring_peers = [lax.rem(group + d, ring) for d in range(1, ring)]
+    chip_peers = [lax.rem(chip + d, chips) * 2 + core for d in range(1, chips)]
+    barrier = pltpu.get_barrier_semaphore()
+    for peer in plane_peers:
+        pl.semaphore_signal(barrier, inc=1, device_id=(group, peer), device_id_type=mesh_type)
+    for peer in ring_peers:
+        pl.semaphore_signal(barrier, inc=1, device_id=(peer, shard), device_id_type=mesh_type)
+    used = [0]
+    sent = []
+
+    def send(src, dst, device):
+        index = used[0]
+        used[0] += 1
+        copy = pltpu.make_async_remote_copy(
+            src_ref=src, dst_ref=dst, send_sem=send_sem.at[index], recv_sem=recv_sem.at[index],
+            device_id=device, device_id_type=mesh_type,
+        )
+        copy.start()
+        sent.append(copy)
+        return copy
+
+    weights[0].wait()
+    projected = jnp.dot(attended_ref[...], w_out[...], preferred_element_type=jnp.float32)
+    for target in range(plane):
+        proj_send[target] = projected[target * steps:(target + 1) * steps].astype(jnp.bfloat16)
+    pl.semaphore_wait(barrier, plane - 1 + ring - 1)
+    copies = [
+        send(proj_send.at[peer], proj_land.at[d], (group, peer))
+        for d, peer in enumerate(plane_peers)
+    ]
+    residual = current_ref[...] + proj_send[shard].astype(jnp.float32)
+    for d, copy in enumerate(copies):
+        copy.wait_recv()
+        residual = residual + proj_land[d].astype(jnp.float32)
+    mlp_all[order, group] = root_mean_scale(residual, gain_ref[...]).astype(jnp.bfloat16)
+
+    own = mlp_all.at[order, group]
+    copies = [send(own, own, (peer, shard)) for peer in ring_peers]
+    for copy in copies:
+        copy.wait_recv()
+    own = mlp_all.at[order]
+    copies = [send(own, own, (group, peer)) for peer in chip_peers]
+    across = [send(own, own, (group, partner))]
+    for d, copy in enumerate(copies):
+        copy.wait_recv()
+        came = mlp_all.at[core * chips + lax.rem(chip + chips - (d + 1), chips)]
+        across.append(send(came, came, (group, partner)))
+    for copy in across:
+        copy.wait_recv()
+
+    width = mlp_all.shape[-1]
+    rows = plane * ring * steps
+    mlp_in = mlp_all[...].astype(jnp.float32).reshape(rows, width).astype(jnp.bfloat16)
+    weights[1].wait()
+    gate_part = jnp.dot(mlp_in, w_gate[...], preferred_element_type=jnp.float32)
+    weights[2].wait()
+    up_part = jnp.dot(mlp_in, w_up[...], preferred_element_type=jnp.float32)
+    hidden = (gate_part / (1.0 + jnp.exp(-gate_part)) * up_part).astype(jnp.bfloat16)
+    weights[3].wait()
+    down = jnp.dot(hidden, w_down[...], preferred_element_type=jnp.float32)
+    half = rows // 2
+    half_send[0] = down[:half].astype(jnp.bfloat16)
+    half_send[1] = down[half:].astype(jnp.bfloat16)
+    copy = send(half_send.at[other], half_land, (group, partner))
+    copy.wait_recv()
+    both = half_send[core].astype(jnp.float32) + half_land[...].astype(jnp.float32)
+    quad = ring * steps
+    for target in range(chips):
+        quad_send[target] = both[target * quad:(target + 1) * quad].astype(jnp.bfloat16)
+    copies = [
+        send(quad_send.at[peer // 2], quad_land.at[d], (group, peer))
+        for d, peer in enumerate(chip_peers)
+    ]
+    summed = quad_send[chip].astype(jnp.float32)
+    for d, copy in enumerate(copies):
+        copy.wait_recv()
+        summed = summed + quad_land[d].astype(jnp.float32)
+    for target in range(ring):
+        ring_send[target] = summed[target * steps:(target + 1) * steps].astype(jnp.bfloat16)
+    copies = [
+        send(ring_send.at[peer], ring_land.at[d], (peer, shard)) for d, peer in enumerate(ring_peers)
+    ]
+    total = residual + ring_send[group].astype(jnp.float32)
+    for d, copy in enumerate(copies):
+        copy.wait_recv()
+        total = total + ring_land[d].astype(jnp.float32)
+    final[shard] = total.astype(jnp.bfloat16)
+    own = final.at[shard]
+    copies = [send(own, own, (group, peer)) for peer in plane_peers]
+    for copy in copies:
+        copy.wait_recv()
+    out_ref[...] = final[...]
+    for copy in sent:
+        copy.wait_send()
+
+
+def run_tail(attended, current, mlp_gain, w_out, w_gate, w_up, w_down, ring, plane, steps):
+    width = w_out.shape[1]
+    rows = plane * ring * steps
+    chips = plane // 2
+    bf16 = jnp.bfloat16
+    copies = 3 * (plane - 1) + 3 * (ring - 1) + 3 * chips + 4
+    vmem = pl.BlockSpec(memory_space=pltpu.VMEM)
+    anywhere = pl.BlockSpec(memory_space=pl.ANY)
+    return pl.pallas_call(
+        functools.partial(tail_kernel, ring, plane, steps),
+        out_shape=jax.ShapeDtypeStruct((plane, steps, width), bf16),
+        in_specs=[vmem] * 3 + [anywhere] * 4,
+        out_specs=vmem,
+        scratch_shapes=[
+            pltpu.VMEM(w_out.shape, bf16),
+            pltpu.VMEM(w_gate.shape, bf16),
+            pltpu.VMEM(w_up.shape, bf16),
+            pltpu.VMEM(w_down.shape, bf16),
+            pltpu.VMEM((plane, steps, width), bf16),
+            pltpu.VMEM((plane - 1, steps, width), bf16),
+            pltpu.VMEM((plane, ring, steps, width), bf16),
+            pltpu.VMEM((2, rows // 2, width), bf16),
+            pltpu.VMEM((rows // 2, width), bf16),
+            pltpu.VMEM((chips, ring * steps, width), bf16),
+            pltpu.VMEM((chips - 1, ring * steps, width), bf16),
+            pltpu.VMEM((ring, steps, width), bf16),
+            pltpu.VMEM((ring - 1, steps, width), bf16),
+            pltpu.VMEM((plane, steps, width), bf16),
+            pltpu.SemaphoreType.DMA((4,)),
+            pltpu.SemaphoreType.DMA((copies,)),
+            pltpu.SemaphoreType.DMA((copies,)),
+        ],
+        compiler_params=pltpu.CompilerParams(collective_id=0, has_side_effects=True),
+    )(attended, current, mlp_gain, w_out, w_gate, w_up, w_down)
 
 
 def body(
@@ -179,28 +332,36 @@
     numer = jnp.sum(factor[..., None] * outs, axis=0)
     denom = jnp.sum(factor * stats[..., 1], axis=0)
     attended = (numer / denom[..., None]).astype(jnp.bfloat16).reshape(all_rows, wide_out)
-    projected = lax.psum_scatter(
-        jnp.dot(attended, w_out, preferred_element_type=jnp.float32),
-        "seq",
-        scatter_dimension=0,
-        tiled=True,
-    )
+    group_count = lax.axis_size("req")
     rows_here = all_rows // shard_count
-    residual = projected + lax.dynamic_slice_in_dim(current, shard_id * rows_here, rows_here, 0)
-    mlp_in = root_mean_scale(residual, mlp_gain).astype(jnp.bfloat16)
-    piece = lax.all_gather(mlp_in, ("req", "seq"), axis=0, tiled=True)
-    gate_part = jnp.dot(piece, w_gate, preferred_element_type=jnp.float32)
-    up_part = jnp.dot(piece, w_up, preferred_element_type=jnp.float32)
-    hidden = (jax.nn.silu(gate_part) * up_part).astype(jnp.bfloat16)
-    down = lax.psum_scatter(
-        jnp.dot(hidden, w_down, preferred_element_type=jnp.float32),
-        ("req", "seq"),
-        scatter_dimension=0,
-        tiled=True,
-    )
-    finished = (residual + down).astype(jnp.bfloat16)
-    outputs = lax.all_gather(finished, "seq", axis=0, tiled=True)
-    outputs = outputs.reshape(row_count, step_count, model_width)
+    if row_count == shard_count and shard_count % 2 == 0:
+        own_rows = lax.dynamic_slice_in_dim(current, shard_id * rows_here, rows_here, 0)
+        outputs = run_tail(
+            attended, own_rows, mlp_gain.reshape(1, -1), w_out, w_gate, w_up, w_down,
+            group_count, shard_count, step_count,
+        )
+    else:
+        projected = lax.psum_scatter(
+            jnp.dot(attended, w_out, preferred_element_type=jnp.float32),
+            "seq",
+            scatter_dimension=0,
+            tiled=True,
+        )
+        residual = projected + lax.dynamic_slice_in_dim(current, shard_id * rows_here, rows_here, 0)
+        mlp_in = root_mean_scale(residual, mlp_gain).astype(jnp.bfloat16)
+        piece = lax.all_gather(mlp_in, ("req", "seq"), axis=0, tiled=True)
+        gate_part = jnp.dot(piece, w_gate, preferred_element_type=jnp.float32)
+        up_part = jnp.dot(piece, w_up, preferred_element_type=jnp.float32)
+        hidden = (jax.nn.silu(gate_part) * up_part).astype(jnp.bfloat16)
+        down = lax.psum_scatter(
+            jnp.dot(hidden, w_down, preferred_element_type=jnp.float32),
+            ("req", "seq"),
+            scatter_dimension=0,
+            tiled=True,
+        )
+        finished = (residual + down).astype(jnp.bfloat16)
+        outputs = lax.all_gather(finished, "seq", axis=0, tiled=True)
+        outputs = outputs.reshape(row_count, step_count, model_width)
     stacked_incoming = jnp.concatenate([incoming_keys, incoming_values], axis=-1)
     appended = jnp.where(owned_here[..., None], stacked_incoming, jnp.zeros((), jnp.bfloat16))
     return (outputs, appended[:, None])

time: 348 us -> 124 us (0.36)
  waiting for transfers between devices: 177 us -> 0.53 us
  blocking collectives: 96.6 us -> 29.2 us
  Pallas kernels: 15.1 us -> 50.2 us
  between operations: 15 us -> 0.96 us
  matrix products: 13.9 us -> 1.97 us
  local copies, waits for them, and re-layouts: 19.9 us -> 27.8 us
    unnamed x4 -> x0, waiting for transfers between devices: 177 us -> none
    all_gather x2 -> x0, blocking collectives: 53.6 us -> none  [the longest x1 44.4 us: body(): piece = lax.all_gather(mlp_in, ('req', 'seq'), axis=0, tiled=True)]
    pallas_call x0 -> x1, Pallas kernels: none -> 35.1 us  [run_tail(): pl.pallas_call(functools.partial(tail_kernel, ring, plane, steps), out_sh...]
    all_to_all x1 -> x0, blocking collectives: 13.7 us -> none  [body(): lax.all_to_all(payload, 'seq', split_axis=1, concat_axis=0, tiled=False)]
    dot_general x3 -> x0, matrix products: 7.96 us -> none  [the longest x1 4.68 us: body(): jnp.dot(hidden, w_down, preferred_element_type=jnp.float32)]
    unnamed x27, local copies, waits for them, and re-layouts: 7.29 us -> 13.6 us
    dot_general x3, matrix products: 4.91 us -> 0.97 us  [body(): jnp.dot(normed, matrix, preferred_element_type=jnp.float32)]
    all_to_all x0 -> x1, starting transfers between devices: none -> 3.54 us  [body(): lax.all_to_all(payload, 'seq', split_axis=1, concat_axis=0, tiled=False)]
  transfers between devices with their start and end apart: 2 -> 1, of which waited for: 2 -> 1; matrix products, arithmetic and copies ran while one was open for 1% -> 9% of each run, Pallas kernels for 0% -> 0%
where the time goes in v1:
time: 124 us; the launch traced here: 123 us
  Pallas kernels  50.2 us (40%)
  blocking collectives  29.2 us (24%)
  local copies, waits for them, and re-layouts  27.8 us (22%)
  other arithmetic  8.33 us (7%)
  starting transfers between devices  3.54 us (3%)
  matrix products  1.97 us (2%)
    pallas_call x1, Pallas kernels, run_tail(): pl.pallas_call(functools.partial(tail_kernel, ring, plane, steps), out_sh...  35.1 us
    all_gather x1, blocking collectives, body(): arrived = lax.all_gather(tokens, 'req', axis=0, tiled=True)  19.6 us
    pallas_call x1, Pallas kernels, body(): pl.pallas_call(functools.partial(attention_kernel, kv_heads, query_heads)...  15.1 us
    unnamed x27, local copies, waits for them, and re-layouts  13.6 us
    all_gather x1, blocking collectives, body(): gathered = lax.all_gather(jnp.concatenate(parts, axis=1), 'seq', axis=0)  9.59 us
    all_to_all x1, starting transfers between devices, body(): lax.all_to_all(payload, 'seq', split_axis=1, concat_axis=0, tiled=False)  3.54 us
    another operation x2, local copies, waits for them, and re-layouts, body(): split(block_out).reshape(all_rows, shard_count, -1)  3.25 us
  transfers between devices with their start and end apart: 1, of which 1 were waited for; matrix products, arithmetic and copies ran while one was open for 9% of the time, Pallas kernels for 0%

profile of v1, /device:TPU:0, one launch (start us, length us, event | category | flops | bytes accessed | tf_op | source)
XLA Modules:
  0.0 122.6 jit_solution(5723552876005689431)
XLA Ops:
  0.6 0.0 copy-start
  0.6 0.0 copy-start.5
  0.7 1.1 copy.69
  1.8 19.6 %all_gather.9 = bf16[32,4,2560]{2,0,1:T(8,128)(2,1)S(1)} all-gather(bf16[8,4,2560]{2,0,1:T(8,128)(2,1)S(1)} %copy.69), channel_id=1, replica_groups=mesh['req'=4,'seq'=8] {'req'}, dimensions={0}, use_global_device_ids=true | all-gather | bytes 819200 | tf_op jit(solution)/shard_map/all_gather | solution.py:259
  21.4 1.0 multiply_reduce_fusion.1
  22.4 0.2 copy.70
  22.6 0.1 reshape.169
  22.8 0.0 copy-start.1
  22.8 0.1 copy.71
  22.9 0.1 rsqrt.31
  23.0 0.0 copy-start.3
  23.0 0.1 multiply_convert_fusion
  23.1 0.5 convolution_convert_fusion
  23.6 0.4 copy-done.2
  24.0 0.2 convolution_convert_fusion.1
  24.3 0.0 copy-done.3
  24.3 0.2 convolution_convert_fusion.2
  24.5 0.0 copy-done.1
  24.5 0.0 copy-start.9
  24.5 0.0 copy-start.7
  24.5 9.6 %all-gather = bf16[256,768]{1,0:T(8,128)(2,1)S(1)} all-gather(bf16[32,768]{1,0:T(8,128)(2,1)S(1)} %pad_maximum_fusion.2), channel_id=2, replica_groups=mesh['req'=4,'seq'=8] {'seq'}, dimensions={0}, use_global_device_ids=true | all-gather | bytes 442368 | tf_op jit(solution)/shard_map/all_gather | solution.py:270
  34.1 0.2 copy.87
  34.4 0.8 slice_convert_fusion
  35.2 0.1 multiply_reduce_fusion.2
  35.3 0.0 copy-start.8
  35.4 1.1 reshape.176
  36.4 0.2 multiply_reduce_fusion
  36.7 0.1 add_convert_fusion.2
  36.8 0.2 multiply_multiply_fusion
  37.0 0.2 multiply_cosine_fusion
  37.2 0.2 subtract_convert_fusion
  37.4 0.1 multiply_multiply_fusion.1
  37.6 0.1 subtract_convert_fusion.1
  37.7 0.1 pad_maximum_fusion.1
  37.8 0.0 copy-start.6
  37.8 1.6 %pad.16.fk_ref = bf16[8,128,1024]{2,1,0:T(8,128)(2,1)} pad(bf16[8,4,1024]{2,1,0:T(4,128)(2,1)S(1)} %convert_element_type.66, bf16[]{:T(256)} %constant.41.clone.1), padding=0_0x0_124x0_0 | pad | bytes 2162690 | tf_op jit(solution)/shard_map/jit(_pad)/pad | solution.py:314
  39.4 1.6 %pad.17.fv_ref = bf16[8,128,1024]{2,1,0:T(8,128)(2,1)} pad(bf16[8,4,1024]{2,1,0:T(4,128)(2,1)S(1)} %reshape.170, bf16[]{:T(256)} %constant.41.clone.1), padding=0_0x0_124x0_0 | pad | bytes 2162690 | tf_op jit(solution)/shard_map/jit(_pad)/pad | solution.py:315
  41.0 0.1 copy.68
  41.1 0.5 broadcast_subtract_fusion.here_ref
  41.6 0.9 pad_maximum_fusion.q_ref
  42.5 0.6 broadcast_in_dim.12.live_ref
  43.1 15.1 %shard_map.176 = (f32[8,128,128]{2,1,0:T(8,128)}, f32[8,128,128]{2,1,0:T(8,128)}, f32[8,128,128]{2,1,0:T(8,128)}) custom-call(s32[8]{0:T(128)} %broadcast_subtract_fusion.here_ref, s32[8,8,128]{2,1,0:T(8,128)} %broadcast_in_dim.12.live_ref, bf16[8,128,128]{2,1,0:T(8,128)(2,1)} %pad_maximum_fusion.q_ref, bf16[8,512,1024]{2,1,0:T(8,128)(2,1)} %k_ref.1, ...), custom_call_target="tpu_custom_call" | custom-call | tf_op jit(solution)/shard_map/pallas_call | solution.py:292
  58.2 1.9 %reshape_reshape.3 = f32[32,8,512]{2,1,0:T(8,128)} reshape(f32[8,128,128]{2,1,0:T(8,128)} %get-tuple-element.5) | data formatting | bytes 1048576 | tf_op jit(solution)/shard_map/reshape;reshape | solution.py:321
  60.1 1.3 %copy.75 = f32[32,8,512]{2,0,1:T(8,128)S(1)} copy(f32[32,8,512]{2,1,0:T(8,128)} %reshape_reshape.3) | data formatting | bytes 1048576 | tf_op jit(solution)/shard_map/reshape;reshape | solution.py:321
  61.5 1.4 %copy.82 = f32[32,8,4,1]{0,1,3,2:T(8,128)S(1)} copy(f32[32,8,4,1]{3,2,1,0:T(4,128)} %bitcast.67) | data formatting | bytes 8192
  62.8 1.4 %copy.83 = f32[32,8,4,1]{0,1,3,2:T(8,128)S(1)} copy(f32[32,8,4,1]{3,2,1,0:T(4,128)} %bitcast.66) | data formatting | bytes 8192
  64.2 0.1 copy.76
  64.3 0.9 maximum_bitcast_fusion
  65.2 3.5 %all-to-all-start = ((f32[1,32,8,520]{3,1,0,2:T(8,128)}), f32[1,32,8,520]{3,1,0,2:T(8,128)S(1)}, u32[]{:S(2)}, u32[]{:S(2)}) async-start(f32[1,32,8,520]{3,1,0,2:T(8,128)} %maximum_bitcast_fusion), calls=%async_computation | async-start | bytes 1310720 | tf_op jit(solution)/shard_map/all_to_all | solution.py:326
  68.8 1.5 %constant_dynamic-slice_fusion.current_ref = f32[4,2560]{1,0:T(4,128)} fusion(f32[32,2560]{1,0:T(8,128)} %copy-done.1, s32[]{:T(128)S(6)} %select_n.14), kind=kLoop, calls=%fused_computation.48 | loop fusion | bytes 81924 | tf_op jit(solution)/shard_map/dynamic_slice | solution.py:338
  70.3 3.8 %copy.80.gate_hbm = bf16[2560,304]{1,0:T(8,128)(2,1)} copy(bf16[2560,304]{0,1:T(8,128)(2,1)} %param.31) | data formatting | bytes 3112960 | tf_op args[14]
  74.1 3.8 %copy.81.up_hbm = bf16[2560,304]{1,0:T(8,128)(2,1)} copy(bf16[2560,304]{0,1:T(8,128)(2,1)} %param.32) | data formatting | bytes 3112960 | tf_op args[15]
  77.9 0.6 reshape.175.gain_ref
  78.5 0.8 maximum_select_fusion
  79.3 0.5 all-to-all-done
  79.8 2.0 %copy.77 = f32[1,32,8,520]{1,2,3,0:T(8,128)} copy(f32[1,32,8,520]{3,1,0,2:T(8,128)S(1)} %all-to-all-done) | data formatting | bytes 1064960 | tf_op jit(solution)/shard_map/all_to_all | solution.py:326
  81.9 0.8 slice.62
  82.7 0.1 copy.78
  82.8 2.2 %fusion = f32[32,512]{0,1:T(8,128)S(1)} fusion(f32[8,32,520]{1,0,2:T(8,128)} %bitcast.59, f32[8,32,4]{1,0,2:T(8,128)S(1)} %exponential_bitcast_fusion), kind=kLoop, calls=%fused_computation.1 | loop fusion | flops 245760 | bytes 593920 | tf_op jit(solution)/shard_map/reduce_sum | solution.py:332
  85.0 0.1 copy.79
  85.1 0.1 div.43
  85.2 0.6 fusion.1.attended_ref
  85.8 35.1 %shard_map.177 = bf16[8,4,2560]{2,1,0:T(4,128)(2,1)} custom-call(bf16[32,512]{1,0:T(8,128)(2,1)} %fusion.1.attended_ref, f32[4,2560]{1,0:T(4,128)} %constant_dynamic-slice_fusion.current_ref, f32[1,2560]{1,0:T(1,128)} %reshape.175.gain_ref, bf16[512,2560]{1,0:T(8,128)(2,1)} %w_out_hbm.1, bf16[2560,304]{1,0:T(8,128)(2,1)} %copy.80.gate_hbm, ...), custom_call_target="tpu_custom_call" | custom-call | tf_op jit(solution)/shard_map/pallas_call | solution.py:201
  120.9 1.6 %copy.89 = bf16[8,4,2560]{2,1,0:T(4,128)(2,1)} copy(bf16[8,4,2560]{2,1,0:T(4,128)(2,1)} %shard_map.177) | data formatting | bytes 327680
  (26 shorter events, 0.2 us)
Async XLA Ops:
  0.6 22.4 %copy-start = (bf16[2560,512]{1,0:T(8,128)(2,1)S(1)}, bf16[2560,512]{1,0:T(8,128)(2,1)}, u32[]{:S(2)}) copy-start(bf16[2560,512]{1,0:T(8,128)(2,1)} %param.24) | copy-start | bytes 7864324
  0.6 22.3 %copy-start.5 = (f32[2560]{0:T(1024)S(1)}, f32[2560]{0:T(1024)}, u32[]{:S(2)}) copy-start(f32[2560]{0:T(1024)} %param.23) | copy-start | bytes 30724
  22.8 1.7 %copy-start.1 = (f32[32,2560]{1,0:T(8,128)}, f32[32,2560]{1,0:T(8,128)S(1)}, u32[]{:S(2)}) copy-start(f32[32,2560]{1,0:T(8,128)S(1)} %reshape.169) | copy-start | bytes 983044
  22.9 1.1 copy-start.2
  23.0 1.3 %copy-start.3 = (bf16[2560,128]{1,0:T(8,128)(2,1)S(1)}, bf16[2560,128]{1,0:T(8,128)(2,1)}, u32[]{:S(2)}) copy-start(bf16[2560,128]{1,0:T(8,128)(2,1)} %param.25) | copy-start | bytes 1966084
  24.5 12.2 %copy-start.9 = (s32[8]{0:T(128)S(1)}, s32[8]{0:T(128)}, u32[]{:S(2)}) copy-start(s32[8]{0:T(128)} %param.19) | copy-start | bytes 100
  24.5 12.3 %copy-start.7 = (f32[128]{0:T(128)S(1)}, f32[128]{0:T(128)}, u32[]{:S(2)}) copy-start(f32[128]{0:T(128)} %param.27) | copy-start | bytes 1540
  35.3 2.1 %copy-start.8 = (f32[128]{0:T(128)S(1)}, f32[128]{0:T(128)}, u32[]{:S(2)}) copy-start(f32[128]{0:T(128)} %param.28) | copy-start | bytes 1540
  37.8 3.2 %copy-start.6 = (s32[8,4]{0,1:T(4,128)S(1)}, s32[8,4]{0,1:T(4,128)}, u32[]{:S(2)}) copy-start(s32[8,4]{0,1:T(4,128)} %param.20) | copy-start | bytes 388
  65.2 14.6 %all-to-all-start = ((f32[1,32,8,520]{3,1,0,2:T(8,128)}), f32[1,32,8,520]{3,1,0,2:T(8,128)S(1)}, u32[]{:S(2)}, u32[]{:S(2)}) async-start(f32[1,32,8,520]{3,1,0,2:T(8,128)} %maximum_bitcast_fusion), calls=%async_computation | async-start | bytes 1310720 | tf_op jit(solution)/shard_map/all_to_all | solution.py:326
  74.1 3.8 %copy-start.4 = (f32[2560]{0:T(1024)S(1)}, f32[2560]{0:T(1024)}, u32[]{:S(2)}) copy-start(f32[2560]{0:T(1024)} %param.30) | copy-start | bytes 30724

commit v2 on v1

--- a/solution.py
+++ b/solution.py
@@ -73,9 +73,13 @@
     sum_ref[0] = jnp.broadcast_to(total, (rows, head_dim))
 
 
-def tail_kernel(ring, plane, steps, attended_ref, current_ref, gain_ref, w_out_hbm, gate_hbm, up_hbm,
-                down_hbm, out_ref, w_out, w_gate, w_up, w_down, proj_send, proj_land, mlp_all, half_send,
-                half_land, quad_send, quad_land, ring_send, ring_land, final, weight_sem, send_sem, recv_sem):
+def layer_kernel(ring, plane, steps, slot_ref, length_ref, owner_ref, tokens_ref, attn_gain_ref, query_gain_ref,
+                 key_gain_ref, cosine_ref, sine_ref, gain_ref, query_hbm, key_hbm, value_hbm, keys_hbm, stored_hbm,
+                 w_out_hbm, gate_hbm, up_hbm, down_hbm, out_ref, incoming_ref, w_query, w_key, w_value, keys, stored,
+                 w_out, w_gate, w_up, w_down, raw_send, raw_land, token_send, token_land, fresh, part_send,
+                 part_land, stat_send, stat_land, proj_send, proj_land, mlp_all, half_send,
+                 half_land, quad_send, quad_land, ring_send, ring_land, final, weight_sem, cache_sem, send_sem,
+                 recv_sem):
     group = lax.axis_index("req")
     shard = lax.axis_index("seq")
     chips = plane // 2
@@ -84,15 +88,10 @@
     partner = chip * 2 + other
     order = core * chips + chip
     mesh_type = pl.DeviceIdType.MESH
-
-    weights = [
-        pltpu.make_async_copy(src, dst, weight_sem.at[i])
-        for i, (src, dst) in enumerate(
-            ((w_out_hbm, w_out), (gate_hbm, w_gate), (up_hbm, w_up), (down_hbm, w_down))
-        )
-    ]
-    for copy in weights:
-        copy.start()
+    bf16, f32 = jnp.bfloat16, jnp.float32
+    nt = (((1,), (1,)), ((), ()))
+    iota = lambda shape, axis: lax.broadcasted_iota(jnp.int32, shape, axis)
+
     plane_peers = [lax.rem(shard + d, plane) for d in range(1, plane)]
     ring_peers = [lax.rem(group + d, ring) for d in range(1, ring)]
     chip_peers = [lax.rem(chip + d, chips) * 2 + core for d in range(1, chips)]
@@ -101,6 +100,31 @@
         pl.semaphore_signal(barrier, inc=1, device_id=(group, peer), device_id_type=mesh_type)
     for peer in ring_peers:
         pl.semaphore_signal(barrier, inc=1, device_id=(peer, shard), device_id_type=mesh_type)
+    loads = [
+        pltpu.make_async_copy(src, dst, weight_sem.at[i])
+        for i, (src, dst) in enumerate(
+            (
+                (query_hbm, w_query), (key_hbm, w_key), (value_hbm, w_value),
+                (w_out_hbm, w_out), (gate_hbm, w_gate), (up_hbm, w_up), (down_hbm, w_down),
+            )
+        )
+    ]
+    slots = keys.shape[0]
+    cached = [
+        (
+            pltpu.make_async_copy(keys_hbm.at[j], keys.at[j], cache_sem.at[0, j]),
+            pltpu.make_async_copy(stored_hbm.at[j], stored.at[j], cache_sem.at[1, j]),
+        )
+        for j in range(slots)
+    ]
+    for copy in loads[:3]:
+        copy.start()
+    for pair in cached:
+        pair[0].start()
+        pair[1].start()
+    for copy in loads[3:]:
+        copy.start()
+    weights = loads[3:]
     used = [0]
     sent = []
 
@@ -115,16 +139,169 @@
         sent.append(copy)
         return copy
 
+    local, _, width = tokens_ref.shape
+    head_dim = query_gain_ref.shape[1]
+    rows = slots * steps
+    group_size = w_query.shape[1] // head_dim
+    flat = tokens_ref[...].astype(f32).reshape(local * steps, width)
+    normed = root_mean_scale(flat, attn_gain_ref[...]).astype(bf16)
+    flat = flat.astype(bf16)
+    tall, short = ring * rows, ring * steps
+    slot_row, slot_lane = iota((tall, local * steps), 0), iota((tall, local * steps), 1)
+    own_row, own_lane = iota((short, local * steps), 0), iota((short, local * steps), 1)
+    pick = jnp.zeros((tall, local * steps), f32)
+    pick_own = jnp.zeros((short, local * steps), f32)
+    for i in range(local):
+        slot = slot_ref[group * local + i]
+        pick = jnp.where((slot_lane // steps == i) & (slot_row // steps == slot), 1.0, pick)
+        pick_own = jnp.where(
+            (own_lane // steps == i) & (own_row // steps * slots + shard == slot), 1.0, pick_own
+        )
+    pick = jnp.where(slot_row % steps == slot_lane % steps, pick, 0.0).astype(bf16)
+    pick_own = jnp.where(own_row % steps == own_lane % steps, pick_own, 0.0).astype(bf16)
+    raw = []
+    for copy, matrix in zip(loads[:3], (w_query, w_key, w_value)):
+        copy.wait()
+        raw.append(jnp.dot(normed, matrix[...], preferred_element_type=f32).astype(bf16))
+    raw = jnp.dot(pick, jnp.concatenate(raw, axis=1), preferred_element_type=f32).astype(bf16)
+    for target in range(ring):
+        raw_send[target] = raw[target * rows:(target + 1) * rows]
+    pl.semaphore_wait(barrier, plane - 1 + ring - 1)
+    copies = [send(raw_send.at[peer], raw_land.at[d], (peer, shard)) for d, peer in enumerate(ring_peers)]
+    chosen = jnp.dot(pick_own, flat, preferred_element_type=f32)
+    for target in range(ring):
+        token_send[target] = chosen[target * steps:(target + 1) * steps].astype(bf16)
+    token_copies = [
+        send(token_send.at[peer], token_land.at[d], (peer, shard)) for d, peer in enumerate(ring_peers)
+    ]
+    raw = raw_send[group].astype(f32)
+    for d, copy in enumerate(copies):
+        copy.wait_recv()
+        raw = raw + raw_land[d].astype(f32)
+    cosine, sine = cosine_ref[...], sine_ref[...]
+
+    def turned(tensor, gain_vec):
+        scaled = root_mean_scale(tensor, gain_vec)
+        return scaled * cosine + pltpu.roll(scaled, head_dim // 2, 1) * sine
+
+    heads = [turned(raw[:, g * head_dim:(g + 1) * head_dim], query_gain_ref[...]) for g in range(group_size)]
+    packed = rows * group_size
+    by_head = jnp.concatenate(heads, axis=0).astype(bf16)
+    row, lane = iota((packed, packed), 0), iota((packed, packed), 1)
+    swap = jnp.where(lane == row % group_size * rows + row // group_size, 1.0, 0.0).astype(bf16)
+    back = jnp.where(lane == row % rows * group_size + row // rows, 1.0, 0.0).astype(bf16)
+    fresh[order, :packed] = jnp.dot(swap, by_head, preferred_element_type=f32).astype(bf16)
+    key_at, value_at = packed, packed + rows
+    wide = group_size * head_dim
+    fresh[order, key_at:value_at] = turned(raw[:, wide:wide + head_dim], key_gain_ref[...]).astype(bf16)
+    fresh[order, value_at:] = raw[:, wide + head_dim:].astype(bf16)
+    own = fresh.at[order]
+    copies = [send(own, own, (group, peer)) for peer in chip_peers]
+    across = [send(own, own, (group, partner))]
+    for d, copy in enumerate(copies):
+        copy.wait_recv()
+        came = fresh.at[core * chips + lax.rem(chip + chips - (d + 1), chips)]
+        across.append(send(came, came, (group, partner)))
+    for copy in across:
+        copy.wait_recv()
+
+    place = [(k % 2) * chips + k // 2 for k in range(plane)]
+    new_keys = jnp.concatenate([fresh[p, key_at:value_at] for p in place], axis=1)
+    new_values = jnp.concatenate([fresh[p, value_at:] for p in place], axis=1)
+    incoming_ref[:, :plane * head_dim] = new_keys
+    incoming_ref[:, plane * head_dim:] = new_values
+    span = keys.shape[1]
+    block = steps * group_size
+    scale = 1.0 / math.sqrt(head_dim)
+    all_queries = plane * block
+    position = iota((all_queries, span), 1)
+    step_row = iota((all_queries, rows), 0) % block // group_size
+    fresh_lane = iota((all_queries, rows), 1)
+    stat_lane = iota((all_queries, 128), 1)
+    stats = jnp.zeros((all_queries, 128), f32)
+    empty = jnp.zeros((block, head_dim), bf16)
+    pair_dim = 2 * head_dim
+    halves = 2
+    part_copies = []
+    for j in range(slots):
+        cached[j][0].wait()
+        pieces, new_pieces = [], []
+        for k in range(0, plane, 2):
+            first = fresh[place[k], j * block:(j + 1) * block]
+            second = fresh[place[k + 1], j * block:(j + 1) * block]
+            both = jnp.concatenate(
+                [jnp.concatenate([first, empty], axis=1), jnp.concatenate([empty, second], axis=1)], axis=0
+            )
+            lanes = slice(k * head_dim, k * head_dim + pair_dim)
+            pieces.append(lax.dot_general(both, keys[j, :, lanes], nt, preferred_element_type=f32))
+            new_pieces.append(lax.dot_general(both, new_keys[:, lanes], nt, preferred_element_type=f32))
+        in_cache = position < length_ref[j] - shard * span
+        scores = jnp.where(in_cache, jnp.concatenate(pieces, axis=0) * scale, MASKED)
+        live = fresh_lane < 0
+        for t in range(steps):
+            target = jnp.where(owner_ref[j, t] == shard, j * steps + t, -1)
+            live = live | ((fresh_lane == target) & (step_row >= t))
+        new_scores = jnp.where(live, jnp.concatenate(new_pieces, axis=0) * scale, MASKED)
+        top = jnp.maximum(
+            jnp.max(scores, axis=1, keepdims=True), jnp.max(new_scores, axis=1, keepdims=True)
+        )
+        portions = jnp.where(in_cache, jnp.exp(scores - top), 0.0)
+        new_portions = jnp.where(live, jnp.exp(new_scores - top), 0.0)
+        total = jnp.sum(portions, axis=1, keepdims=True) + jnp.sum(new_portions, axis=1, keepdims=True)
+        portions, new_portions = portions.astype(bf16), new_portions.astype(bf16)
+        stats = jnp.where(stat_lane == j, top, jnp.where(stat_lane == slots + j, total, stats))
+        cached[j][1].wait()
+        for k in range(0, plane, 2):
+            lanes = slice(k * head_dim, k * head_dim + pair_dim)
+            span_rows = slice(k * block, (k + 2) * block)
+            product = jnp.dot(portions[span_rows], stored[j, :, lanes], preferred_element_type=f32)
+            product = product + jnp.dot(
+                new_portions[span_rows], new_values[:, lanes], preferred_element_type=f32
+            )
+            at = slice(j * block, (j + 1) * block)
+            part_send[k, at] = product[:block, :head_dim].astype(bf16)
+            part_send[k + 1, at] = product[block:, head_dim:].astype(bf16)
+        if (j + 1) % (slots // halves) == 0:
+            cut = pl.ds((j + 1 - slots // halves) * block, slots // halves * block)
+            for d, peer in enumerate(plane_peers):
+                part_copies.append(
+                    send(part_send.at[peer, cut], part_land.at[d, cut], (group, peer))
+                )
+    stat_send[...] = jnp.transpose(stats)[:2 * slots]
+    stat_copies = [send(stat_send, stat_land.at[d], (group, peer)) for d, peer in enumerate(plane_peers)]
+    for copy in stat_copies:
+        copy.wait_recv()
+    tops = [stat_send[:slots]] + [stat_land[d, :slots] for d in range(plane - 1)]
+    sums = [stat_send[slots:]] + [stat_land[d, slots:] for d in range(plane - 1)]
+    joint = functools.reduce(jnp.maximum, tops)
+    factors = [jnp.exp(value - joint) for value in tops]
+    denom = functools.reduce(jnp.add, [f * s for f, s in zip(factors, sums)])
+    here = iota((packed, 128), 1) == iota((packed, 128), 0) % block + shard * block
+    columns = []
+    for factor in factors:
+        spread = jnp.broadcast_to((factor / denom)[:, None, :], (slots, block, 128)).reshape(packed, 128)
+        columns.append(jnp.sum(jnp.where(here, spread, 0.0), axis=1, keepdims=True))
+    for copy in part_copies:
+        copy.wait_recv()
+    blended = columns[0] * part_send[shard].astype(f32)
+    for d in range(plane - 1):
+        blended = blended + columns[d + 1] * part_land[d].astype(f32)
+    blended = jnp.dot(back, blended.astype(bf16), preferred_element_type=f32).astype(bf16)
+    attended = jnp.concatenate([blended[g * rows:(g + 1) * rows] for g in range(group_size)], axis=1)
+    current = token_send[group].astype(f32)
+    for d, copy in enumerate(token_copies):
+        copy.wait_recv()
+        current = current + token_land[d].astype(f32)
+
     weights[0].wait()
-    projected = jnp.dot(attended_ref[...], w_out[...], preferred_element_type=jnp.float32)
+    projected = jnp.dot(attended, w_out[...], preferred_element_type=jnp.float32)
     for target in range(plane):
         proj_send[target] = projected[target * steps:(target + 1) * steps].astype(jnp.bfloat16)
-    pl.semaphore_wait(barrier, plane - 1 + ring - 1)
     copies = [
         send(proj_send.at[peer], proj_land.at[d], (group, peer))
         for d, peer in enumerate(plane_peers)
     ]
-    residual = current_ref[...] + proj_send[shard].astype(jnp.float32)
+    residual = current + proj_send[shard].astype(jnp.float32)
     for d, copy in enumerate(copies):
         copy.wait_recv()
         residual = residual + proj_land[d].astype(jnp.float32)
@@ -148,9 +325,9 @@
     rows = plane * ring * steps
     mlp_in = mlp_all[...].astype(jnp.float32).reshape(rows, width).astype(jnp.bfloat16)
     weights[1].wait()
-    gate_part = jnp.dot(mlp_in, w_gate[...], preferred_element_type=jnp.float32)
+    gate_part = lax.dot_general(mlp_in, w_gate[...], nt, preferred_element_type=jnp.float32)
     weights[2].wait()
-    up_part = jnp.dot(mlp_in, w_up[...], preferred_element_type=jnp.float32)
+    up_part = lax.dot_general(mlp_in, w_up[...], nt, preferred_element_type=jnp.float32)
     hidden = (gate_part / (1.0 + jnp.exp(-gate_part)) * up_part).astype(jnp.bfloat16)
     weights[3].wait()
     down = jnp.dot(hidden, w_down[...], preferred_element_type=jnp.float32)
@@ -190,40 +367,107 @@
         copy.wait_send()
 
 
-def run_tail(attended, current, mlp_gain, w_out, w_gate, w_up, w_down, ring, plane, steps):
+def run_layer(scalars, vectors, matrices, ring, plane, steps):
+    tokens = vectors[0]
+    w_query, key_matrix, value_matrix, cache_keys, stored_values, w_out, w_gate, w_up, w_down = matrices
     width = w_out.shape[1]
-    rows = plane * ring * steps
+    head_dim = key_matrix.shape[1]
+    slots = cache_keys.shape[0]
+    all_rows = plane * ring * steps
+    rows = slots * steps
+    packed = rows * (w_query.shape[1] // head_dim)
+    made = w_query.shape[1] + 2 * head_dim
     chips = plane // 2
-    bf16 = jnp.bfloat16
-    copies = 3 * (plane - 1) + 3 * (ring - 1) + 3 * chips + 4
+    bf16, f32 = jnp.bfloat16, jnp.float32
+    copies = 5 * (plane - 1) + 5 * (ring - 1) + 5 * chips + 8
     vmem = pl.BlockSpec(memory_space=pltpu.VMEM)
+    smem = pl.BlockSpec(memory_space=pltpu.SMEM)
     anywhere = pl.BlockSpec(memory_space=pl.ANY)
     return pl.pallas_call(
-        functools.partial(tail_kernel, ring, plane, steps),
-        out_shape=jax.ShapeDtypeStruct((plane, steps, width), bf16),
-        in_specs=[vmem] * 3 + [anywhere] * 4,
-        out_specs=vmem,
-        scratch_shapes=[
-            pltpu.VMEM(w_out.shape, bf16),
-            pltpu.VMEM(w_gate.shape, bf16),
-            pltpu.VMEM(w_up.shape, bf16),
-            pltpu.VMEM(w_down.shape, bf16),
+        functools.partial(layer_kernel, ring, plane, steps),
+        out_shape=(
+            jax.ShapeDtypeStruct((plane, steps, width), bf16),
+            jax.ShapeDtypeStruct((rows, 2 * plane * head_dim), bf16),
+        ),
+        in_specs=[smem] * len(scalars) + [vmem] * len(vectors) + [anywhere] * len(matrices),
+        out_specs=(vmem, vmem),
+        scratch_shapes=[pltpu.VMEM(matrix.shape, bf16) for matrix in matrices] + [
+            pltpu.VMEM((ring, rows, made), bf16),
+            pltpu.VMEM((ring - 1, rows, made), bf16),
+            pltpu.VMEM((ring, steps, width), bf16),
+            pltpu.VMEM((ring - 1, steps, width), bf16),
+            pltpu.VMEM((plane, packed + 2 * rows, head_dim), bf16),
+            pltpu.VMEM((plane, packed, head_dim), bf16),
+            pltpu.VMEM((plane - 1, packed, head_dim), bf16),
+            pltpu.VMEM((2 * slots, 128), f32),
+            pltpu.VMEM((plane - 1, 2 * slots, 128), f32),
             pltpu.VMEM((plane, steps, width), bf16),
             pltpu.VMEM((plane - 1, steps, width), bf16),
             pltpu.VMEM((plane, ring, steps, width), bf16),
-            pltpu.VMEM((2, rows // 2, width), bf16),
-            pltpu.VMEM((rows // 2, width), bf16),
+            pltpu.VMEM((2, all_rows // 2, width), bf16),
+            pltpu.VMEM((all_rows // 2, width), bf16),
             pltpu.VMEM((chips, ring * steps, width), bf16),
             pltpu.VMEM((chips - 1, ring * steps, width), bf16),
             pltpu.VMEM((ring, steps, width), bf16),
             pltpu.VMEM((ring - 1, steps, width), bf16),
             pltpu.VMEM((plane, steps, width), bf16),
-            pltpu.SemaphoreType.DMA((4,)),
+            pltpu.SemaphoreType.DMA((7,)),
+            pltpu.SemaphoreType.DMA((2, slots)),
             pltpu.SemaphoreType.DMA((copies,)),
             pltpu.SemaphoreType.DMA((copies,)),
         ],
         compiler_params=pltpu.CompilerParams(collective_id=0, has_side_effects=True),
-    )(attended, current, mlp_gain, w_out, w_gate, w_up, w_down)
+    )(*scalars, *vectors, *matrices)
+
+
+def whole_layer(
+    tokens,
+    slot_of,
+    cache_len,
+    owner_shard,
+    cache_keys,
+    stored_values,
+    attn_gain,
+    w_query,
+    key_matrix,
+    value_matrix,
+    query_gain,
+    key_norm_weight,
+    w_out,
+    mlp_gain,
+    w_gate,
+    w_up,
+    w_down,
+):
+    plane, ring = lax.axis_size("seq"), lax.axis_size("req")
+    slots, steps = owner_shard.shape
+    head_dim = query_gain.shape[0]
+    half = head_dim // 2
+    position = (cache_len[:, None] + jnp.arange(steps, dtype=jnp.int32)).astype(jnp.float32)
+    frequency = ROPE_BASE ** (-2.0 * jnp.arange(half, dtype=jnp.float32) / head_dim)
+    angles = position.reshape(-1, 1) * frequency
+    cosine, sine = jnp.cos(angles), jnp.sin(angles)
+    outputs, incoming = run_layer(
+        (slot_of, cache_len, owner_shard),
+        (
+            tokens,
+            attn_gain.reshape(1, -1),
+            query_gain.reshape(1, -1),
+            key_norm_weight.reshape(1, -1),
+            jnp.concatenate([cosine, cosine], axis=1),
+            jnp.concatenate([-sine, sine], axis=1),
+            mlp_gain.reshape(1, -1),
+        ),
+        (
+            w_query, key_matrix, value_matrix, cache_keys, stored_values, w_out,
+            w_gate.T, w_up.T, w_down,
+        ),
+        ring, plane, steps,
+    )
+    owned_here = owner_shard == lax.axis_index("seq")
+    incoming = incoming.reshape(slots, steps, -1)
+    appended = jnp.where(owned_here[..., None], incoming, jnp.zeros((), jnp.bfloat16))
+    return (outputs, appended[:, None])
 
 
 def body(
@@ -332,36 +576,28 @@
     numer = jnp.sum(factor[..., None] * outs, axis=0)
     denom = jnp.sum(factor * stats[..., 1], axis=0)
     attended = (numer / denom[..., None]).astype(jnp.bfloat16).reshape(all_rows, wide_out)
-    group_count = lax.axis_size("req")
+    projected = lax.psum_scatter(
+        jnp.dot(attended, w_out, preferred_element_type=jnp.float32),
+        "seq",
+        scatter_dimension=0,
+        tiled=True,
+    )
     rows_here = all_rows // shard_count
-    if row_count == shard_count and shard_count % 2 == 0:
-        own_rows = lax.dynamic_slice_in_dim(current, shard_id * rows_here, rows_here, 0)
-        outputs = run_tail(
-            attended, own_rows, mlp_gain.reshape(1, -1), w_out, w_gate, w_up, w_down,
-            group_count, shard_count, step_count,
-        )
-    else:
-        projected = lax.psum_scatter(
-            jnp.dot(attended, w_out, preferred_element_type=jnp.float32),
-            "seq",
-            scatter_dimension=0,
-            tiled=True,
-        )
-        residual = projected + lax.dynamic_slice_in_dim(current, shard_id * rows_here, rows_here, 0)
-        mlp_in = root_mean_scale(residual, mlp_gain).astype(jnp.bfloat16)
-        piece = lax.all_gather(mlp_in, ("req", "seq"), axis=0, tiled=True)
-        gate_part = jnp.dot(piece, w_gate, preferred_element_type=jnp.float32)
-        up_part = jnp.dot(piece, w_up, preferred_element_type=jnp.float32)
-        hidden = (jax.nn.silu(gate_part) * up_part).astype(jnp.bfloat16)
-        down = lax.psum_scatter(
-            jnp.dot(hidden, w_down, preferred_element_type=jnp.float32),
-            ("req", "seq"),
-            scatter_dimension=0,
-            tiled=True,
-        )
-        finished = (residual + down).astype(jnp.bfloat16)
-        outputs = lax.all_gather(finished, "seq", axis=0, tiled=True)
-        outputs = outputs.reshape(row_count, step_count, model_width)
+    residual = projected + lax.dynamic_slice_in_dim(current, shard_id * rows_here, rows_here, 0)
+    mlp_in = root_mean_scale(residual, mlp_gain).astype(jnp.bfloat16)
+    piece = lax.all_gather(mlp_in, ("req", "seq"), axis=0, tiled=True)
+    gate_part = jnp.dot(piece, w_gate, preferred_element_type=jnp.float32)
+    up_part = jnp.dot(piece, w_up, preferred_element_type=jnp.float32)
+    hidden = (jax.nn.silu(gate_part) * up_part).astype(jnp.bfloat16)
+    down = lax.psum_scatter(
+        jnp.dot(hidden, w_down, preferred_element_type=jnp.float32),
+        ("req", "seq"),
+        scatter_dimension=0,
+        tiled=True,
+    )
+    finished = (residual + down).astype(jnp.bfloat16)
+    outputs = lax.all_gather(finished, "seq", axis=0, tiled=True)
+    outputs = outputs.reshape(row_count, step_count, model_width)
     stacked_incoming = jnp.concatenate([incoming_keys, incoming_values], axis=-1)
     appended = jnp.where(owned_here[..., None], stacked_incoming, jnp.zeros((), jnp.bfloat16))
     return (outputs, appended[:, None])
@@ -388,4 +624,13 @@
         P(("req", "seq"), None),
     )
     out_specs = (P("req", None, None), P("req", "seq", None, None))
-    return jax.shard_map(body, mesh=mesh, in_specs=in_specs, out_specs=out_specs, check_vma=False)
+
+    def layer(*arrays):
+        kv_heads = arrays[4].shape[2] // arrays[10].shape[0]
+        row_count = arrays[2].shape[0]
+        shards = lax.axis_size("seq")
+        if row_count == shards and kv_heads == shards and shards % 2 == 0:
+            return whole_layer(*arrays)
+        return body(*arrays)
+
+    return jax.shard_map(layer, mesh=mesh, in_specs=in_specs, out_specs=out_specs, check_vma=False)

time: 124 us -> 78.3 us (0.63)
  blocking collectives: 29.2 us -> 0 us
  local copies, waits for them, and re-layouts: 27.8 us -> 6.74 us
  Pallas kernels: 50.2 us -> 68.2 us
  other arithmetic: 8.33 us -> 2.37 us
  starting transfers between devices: 3.54 us -> 0 us
  matrix products: 1.97 us -> 0 us
    all_gather x2 -> x0, blocking collectives: 29.2 us -> none  [the longest x1 19.6 us: body(): arrived = lax.all_gather(tokens, 'req', axis=0, tiled=True)]
    pallas_call x2 -> x1, Pallas kernels: 50.2 us -> 68.2 us  [run_layer(): pl.pallas_call(functools.partial(layer_kernel, ring, plane, steps), out_s...]
    unnamed x27 -> x4, local copies, waits for them, and re-layouts: 13.6 us -> 2.98 us
    all_to_all x1 -> x0, starting transfers between devices: 3.54 us -> none  [body(): lax.all_to_all(payload, 'seq', split_axis=1, concat_axis=0, tiled=False)]
    another operation x2 -> x0, local copies, waits for them, and re-layouts: 3.25 us -> none  [body(): split(block_out).reshape(all_rows, shard_count, -1)]
    pad x2 -> x0, local copies, waits for them, and re-layouts: 3.17 us -> none  [the longest x1 1.61 us: body(): jnp.pad(incoming_keys, widen)]
    reshape x4 -> x3, local copies, waits for them, and re-layouts: 0.83 us -> 3.58 us  [the longest x1 1.31 us: whole_layer(): mlp_gain.reshape(1, -1)]
    reduce_sum x4 -> x0, other arithmetic: 2.57 us -> none  [the longest x1 2.22 us: body(): numer = jnp.sum(factor[..., None] * outs, axis=0)]
  transfers between devices with their start and end apart: 1 -> 0, of which waited for: 1 -> 0; matrix products, arithmetic and copies ran while one was open for 9% -> 0% of each run, Pallas kernels for 0% -> 0%
where the time goes in v2:
time: 78.3 us; the launch traced here: 77.9 us
  Pallas kernels  68.2 us (87%)
  local copies, waits for them, and re-layouts  6.74 us (9%)
  other arithmetic  2.37 us (3%)
    pallas_call x1, Pallas kernels, run_layer(): pl.pallas_call(functools.partial(layer_kernel, ring, plane, steps), out_s...  68.2 us
    unnamed x4, local copies, waits for them, and re-layouts  2.98 us

profile of v2, /device:TPU:0, one launch (start us, length us, event | category | flops | bytes accessed | tf_op | source)
XLA Modules:
  0.0 77.9 jit_solution(16917130487942479959)
XLA Ops:
  0.6 0.7 add_convert_fusion
  1.4 0.1 convert_element_type.11
  1.4 0.1 fusion
  1.6 0.7 pad_maximum_fusion
  2.3 1.3 %reshape.53.attn_gain_ref = f32[1,2560]{1,0:T(1,128)} reshape(f32[2560]{0:T(1024)} %param.23) | data formatting | bytes 20480 | tf_op jit(solution)/shard_map/reshape | solution.py:454
  3.6 1.3 %reshape.56.gain_ref = f32[1,2560]{1,0:T(1,128)} reshape(f32[2560]{0:T(1024)} %param.30) | data formatting | bytes 20480 | tf_op jit(solution)/shard_map/reshape | solution.py:459
  4.9 1.3 %copy.22.owner_ref = s32[8,4]{1,0:T(8,128)} copy(s32[8,4]{0,1:T(4,128)} %param.20) | data formatting | bytes 256 | tf_op args[3]
  6.3 0.0 copy-start
  6.3 68.2 %shard_map.176 = (bf16[8,4,2560]{2,1,0:T(4,128)(2,1)}, bf16[32,2048]{1,0:T(8,128)(2,1)}) custom-call(s32[32]{0:T(128)} %slot_ref.1, s32[8]{0:T(128)} %length_ref.1, s32[8,4]{1,0:T(8,128)} %copy.22.owner_ref, bf16[8,4,2560]{2,1,0:T(4,128)(2,1)} %tokens_ref.1, f32[1,2560]{1,0:T(1,128)} %reshape.53.attn_gain_ref, f32[1,128]{1,0:T(1,128)} %bitcast.8, ...), custom_call_target="tpu_custom_call" | custom-call | tf_op jit(solution)/shard_map/pallas_call | solution.py:386
  74.4 1.0 %reshape.57 = bf16[8,1,4,2048]{3,2,0,1:T(4,128)(2,1)S(1)} reshape(bf16[32,2048]{1,0:T(8,128)(2,1)} %get-tuple-element.5) | data formatting | bytes 262144 | tf_op jit(solution)/shard_map/reshape | solution.py:468
  75.4 0.0 copy-done
  75.4 0.1 copy.23
  75.5 0.8 %bitcast_select_fusion = bf16[8,1,4,2048]{3,2,1,0:T(4,128)(2,1)} fusion(bf16[8,1,4,2048]{3,2,0,1:T(4,128)(2,1)S(1)} %reshape.57, pred[8,4]{1,0:T(8,128)(4,1)S(1)} %copy.23), kind=kLoop, calls=%fused_computation | loop fusion | flops 65536 | bytes 262176 | tf_op jit(solution)/shard_map/jit(_where)/select_n | solution.py:469
  76.3 1.6 %copy.26 = bf16[8,4,2560]{2,1,0:T(4,128)(2,1)} copy(bf16[8,4,2560]{2,1,0:T(4,128)(2,1)} %get-tuple-element.13) | data formatting | bytes 327680
  (2 shorter events, 0.0 us)
Async XLA Ops:
  6.3 69.1 %copy-start = (s32[8,4]{0,1:T(4,128)S(1)}, s32[8,4]{0,1:T(4,128)}, u32[]{:S(2)}) copy-start(s32[8,4]{0,1:T(4,128)} %param.20) | copy-start | bytes 388

commit v3 on v2

--- a/solution.py
+++ b/solution.py
@@ -73,12 +73,17 @@
     sum_ref[0] = jnp.broadcast_to(total, (rows, head_dim))
 
 
+def unfolded(folded_ref):
+    folded = folded_ref[...]
+    return jnp.concatenate([folded[i:i + 1] for i in range(folded.shape[0])], axis=1)
+
+
 def layer_kernel(ring, plane, steps, slot_ref, length_ref, owner_ref, tokens_ref, attn_gain_ref, query_gain_ref,
                  key_gain_ref, cosine_ref, sine_ref, gain_ref, query_hbm, key_hbm, value_hbm, keys_hbm, stored_hbm,
                  w_out_hbm, gate_hbm, up_hbm, down_hbm, out_ref, incoming_ref, w_query, w_key, w_value, keys, stored,
                  w_out, w_gate, w_up, w_down, raw_send, raw_land, token_send, token_land, fresh, part_send,
-                 part_land, stat_send, stat_land, proj_send, proj_land, mlp_all, half_send,
-                 half_land, quad_send, quad_land, ring_send, ring_land, final, weight_sem, cache_sem, send_sem,
+                 part_land, stat_send, stat_land, proj_send, proj_land, mlp_all, hidden_ref,
+                 half_send, half_land, quad_send, quad_land, ring_send, ring_land, final, weight_sem, cache_sem, send_sem,
                  recv_sem):
     group = lax.axis_index("req")
     shard = lax.axis_index("seq")
@@ -144,7 +149,7 @@
     rows = slots * steps
     group_size = w_query.shape[1] // head_dim
     flat = tokens_ref[...].astype(f32).reshape(local * steps, width)
-    normed = root_mean_scale(flat, attn_gain_ref[...]).astype(bf16)
+    normed = root_mean_scale(flat, unfolded(attn_gain_ref)).astype(bf16)
     flat = flat.astype(bf16)
     tall, short = ring * rows, ring * steps
     slot_row, slot_lane = iota((tall, local * steps), 0), iota((tall, local * steps), 1)
@@ -171,13 +176,13 @@
     chosen = jnp.dot(pick_own, flat, preferred_element_type=f32)
     for target in range(ring):
         token_send[target] = chosen[target * steps:(target + 1) * steps].astype(bf16)
+    raw = raw_send[group].astype(f32)
+    for d, copy in enumerate(copies):
+        copy.wait_recv()
+        raw = raw + raw_land[d].astype(f32)
     token_copies = [
         send(token_send.at[peer], token_land.at[d], (peer, shard)) for d, peer in enumerate(ring_peers)
     ]
-    raw = raw_send[group].astype(f32)
-    for d, copy in enumerate(copies):
-        copy.wait_recv()
-        raw = raw + raw_land[d].astype(f32)
     cosine, sine = cosine_ref[...], sine_ref[...]
 
     def turned(tensor, gain_vec):
@@ -208,8 +213,6 @@
     place = [(k % 2) * chips + k // 2 for k in range(plane)]
     new_keys = jnp.concatenate([fresh[p, key_at:value_at] for p in place], axis=1)
     new_values = jnp.concatenate([fresh[p, value_at:] for p in place], axis=1)
-    incoming_ref[:, :plane * head_dim] = new_keys
-    incoming_ref[:, plane * head_dim:] = new_values
     span = keys.shape[1]
     block = steps * group_size
     scale = 1.0 / math.sqrt(head_dim)
@@ -221,7 +224,7 @@
     stats = jnp.zeros((all_queries, 128), f32)
     empty = jnp.zeros((block, head_dim), bf16)
     pair_dim = 2 * head_dim
-    halves = 2
+    halves = 4
     part_copies = []
     for j in range(slots):
         cached[j][0].wait()
@@ -239,7 +242,7 @@
         scores = jnp.where(in_cache, jnp.concatenate(pieces, axis=0) * scale, MASKED)
         live = fresh_lane < 0
         for t in range(steps):
-            target = jnp.where(owner_ref[j, t] == shard, j * steps + t, -1)
+            target = jnp.where(owner_ref[t, j] == shard, j * steps + t, -1)
             live = live | ((fresh_lane == target) & (step_row >= t))
         new_scores = jnp.where(live, jnp.concatenate(new_pieces, axis=0) * scale, MASKED)
         top = jnp.maximum(
@@ -301,23 +304,32 @@
         send(proj_send.at[peer], proj_land.at[d], (group, peer))
         for d, peer in enumerate(plane_peers)
     ]
+    for at, fresh_rows in ((0, new_keys), (plane * head_dim, new_values)):
+        fresh_rows = fresh_rows.astype(f32)
+        for j in range(slots):
+            incoming_ref[j, :, at:at + plane * head_dim] = fresh_rows[j * steps:(j + 1) * steps].astype(bf16)
     residual = current + proj_send[shard].astype(jnp.float32)
     for d, copy in enumerate(copies):
         copy.wait_recv()
         residual = residual + proj_land[d].astype(jnp.float32)
-    mlp_all[order, group] = root_mean_scale(residual, gain_ref[...]).astype(jnp.bfloat16)
+    mlp_all[order, group] = root_mean_scale(residual, unfolded(gain_ref)).astype(jnp.bfloat16)
 
     own = mlp_all.at[order, group]
-    copies = [send(own, own, (peer, shard)) for peer in ring_peers]
-    for copy in copies:
-        copy.wait_recv()
-    own = mlp_all.at[order]
-    copies = [send(own, own, (group, peer)) for peer in chip_peers]
-    across = [send(own, own, (group, partner))]
-    for d, copy in enumerate(copies):
-        copy.wait_recv()
-        came = mlp_all.at[core * chips + lax.rem(chip + chips - (d + 1), chips)]
-        across.append(send(came, came, (group, partner)))
+    ring_copies = [None] + [send(own, own, (peer, shard)) for peer in ring_peers]
+    spread_copies, across = [], []
+    for d, copy in enumerate(ring_copies):
+        source = lax.rem(group + ring - d, ring)
+        if copy is not None:
+            copy.wait_recv()
+        held = mlp_all.at[order, source]
+        spread_copies.append([send(held, held, (group, peer)) for peer in chip_peers])
+        across.append(send(held, held, (group, partner)))
+    for d, copies in enumerate(spread_copies):
+        source = lax.rem(group + ring - d, ring)
+        for e, copy in enumerate(copies):
+            copy.wait_recv()
+            held = mlp_all.at[core * chips + lax.rem(chip + chips - (e + 1), chips), source]
+            across.append(send(held, held, (group, partner)))
     for copy in across:
         copy.wait_recv()
 
@@ -330,31 +342,39 @@
     up_part = lax.dot_general(mlp_in, w_up[...], nt, preferred_element_type=jnp.float32)
     hidden = (gate_part / (1.0 + jnp.exp(-gate_part)) * up_part).astype(jnp.bfloat16)
     weights[3].wait()
-    down = jnp.dot(hidden, w_down[...], preferred_element_type=jnp.float32)
     half = rows // 2
-    half_send[0] = down[:half].astype(jnp.bfloat16)
-    half_send[1] = down[half:].astype(jnp.bfloat16)
-    copy = send(half_send.at[other], half_land, (group, partner))
+    hidden_ref[0] = hidden[:half]
+    hidden_ref[1] = hidden[half:]
+    half_send[...] = jnp.dot(hidden_ref[other], w_down[...], preferred_element_type=jnp.float32).astype(
+        jnp.bfloat16
+    )
+    copy = send(half_send, half_land, (group, partner))
+    both = jnp.dot(hidden_ref[core], w_down[...], preferred_element_type=jnp.float32)
     copy.wait_recv()
-    both = half_send[core].astype(jnp.float32) + half_land[...].astype(jnp.float32)
-    quad = ring * steps
-    for target in range(chips):
-        quad_send[target] = both[target * quad:(target + 1) * quad].astype(jnp.bfloat16)
-    copies = [
-        send(quad_send.at[peer // 2], quad_land.at[d], (group, peer))
-        for d, peer in enumerate(chip_peers)
+    both = both + half_land[...].astype(jnp.float32)
+    for target in range(chips * ring):
+        quad_send[target // ring, target % ring] = both[target * steps:(target + 1) * steps].astype(
+            jnp.bfloat16
+        )
+    targets = ring_peers + [group]
+    quad_copies = [
+        [
+            send(quad_send.at[peer // 2, target], quad_land.at[e, target], (group, peer))
+            for e, peer in enumerate(chip_peers)
+        ]
+        for target in targets
     ]
-    summed = quad_send[chip].astype(jnp.float32)
-    for d, copy in enumerate(copies):
-        copy.wait_recv()
-        summed = summed + quad_land[d].astype(jnp.float32)
-    for target in range(ring):
-        ring_send[target] = summed[target * steps:(target + 1) * steps].astype(jnp.bfloat16)
-    copies = [
-        send(ring_send.at[peer], ring_land.at[d], (peer, shard)) for d, peer in enumerate(ring_peers)
-    ]
-    total = residual + ring_send[group].astype(jnp.float32)
-    for d, copy in enumerate(copies):
+    ring_copies = []
+    for d, target in enumerate(targets):
+        summed = quad_send[chip, target].astype(jnp.float32)
+        for e, copy in enumerate(quad_copies[d]):
+            copy.wait_recv()
+            summed = summed + quad_land[e, target].astype(jnp.float32)
+        if d < ring - 1:
+            ring_send[d] = summed.astype(jnp.bfloat16)
+            ring_copies.append(send(ring_send.at[d], ring_land.at[d], (target, shard)))
+    total = residual + summed
+    for d, copy in enumerate(ring_copies):
         copy.wait_recv()
         total = total + ring_land[d].astype(jnp.float32)
     final[shard] = total.astype(jnp.bfloat16)
@@ -362,7 +382,7 @@
     copies = [send(own, own, (group, peer)) for peer in plane_peers]
     for copy in copies:
         copy.wait_recv()
-    out_ref[...] = final[...]
+    out_ref[...] = final[...].astype(f32)
     for copy in sent:
         copy.wait_send()
 
@@ -379,15 +399,15 @@
     made = w_query.shape[1] + 2 * head_dim
     chips = plane // 2
     bf16, f32 = jnp.bfloat16, jnp.float32
-    copies = 5 * (plane - 1) + 5 * (ring - 1) + 5 * chips + 8
+    copies = 7 * (plane - 1) + 4 * (ring - 1) + 2 * chips + ring * (3 * chips - 1) + 2
     vmem = pl.BlockSpec(memory_space=pltpu.VMEM)
     smem = pl.BlockSpec(memory_space=pltpu.SMEM)
     anywhere = pl.BlockSpec(memory_space=pl.ANY)
     return pl.pallas_call(
         functools.partial(layer_kernel, ring, plane, steps),
         out_shape=(
-            jax.ShapeDtypeStruct((plane, steps, width), bf16),
-            jax.ShapeDtypeStruct((rows, 2 * plane * head_dim), bf16),
+            jax.ShapeDtypeStruct((plane, steps, width), f32),
+            jax.ShapeDtypeStruct((slots, steps, 2 * plane * head_dim), bf16),
         ),
         in_specs=[smem] * len(scalars) + [vmem] * len(vectors) + [anywhere] * len(matrices),
         out_specs=(vmem, vmem),
@@ -404,11 +424,12 @@
             pltpu.VMEM((plane, steps, width), bf16),
             pltpu.VMEM((plane - 1, steps, width), bf16),
             pltpu.VMEM((plane, ring, steps, width), bf16),
-            pltpu.VMEM((2, all_rows // 2, width), bf16),
+            pltpu.VMEM((2, all_rows // 2, w_down.shape[0]), bf16),
             pltpu.VMEM((all_rows // 2, width), bf16),
-            pltpu.VMEM((chips, ring * steps, width), bf16),
-            pltpu.VMEM((chips - 1, ring * steps, width), bf16),
-            pltpu.VMEM((ring, steps, width), bf16),
+            pltpu.VMEM((all_rows // 2, width), bf16),
+            pltpu.VMEM((chips, ring, steps, width), bf16),
+            pltpu.VMEM((chips - 1, ring, steps, width), bf16),
+            pltpu.VMEM((ring - 1, steps, width), bf16),
             pltpu.VMEM((ring - 1, steps, width), bf16),
             pltpu.VMEM((plane, steps, width), bf16),
             pltpu.SemaphoreType.DMA((7,)),
@@ -448,15 +469,15 @@
     angles = position.reshape(-1, 1) * frequency
     cosine, sine = jnp.cos(angles), jnp.sin(angles)
     outputs, incoming = run_layer(
-        (slot_of, cache_len, owner_shard),
+        (slot_of, cache_len, owner_shard.T),
         (
             tokens,
-            attn_gain.reshape(1, -1),
+            attn_gain.reshape(-1, 128),
             query_gain.reshape(1, -1),
             key_norm_weight.reshape(1, -1),
             jnp.concatenate([cosine, cosine], axis=1),
             jnp.concatenate([-sine, sine], axis=1),
-            mlp_gain.reshape(1, -1),
+            mlp_gain.reshape(-1, 128),
         ),
         (
             w_query, key_matrix, value_matrix, cache_keys, stored_values, w_out,
@@ -465,9 +486,8 @@
         ring, plane, steps,
     )
     owned_here = owner_shard == lax.axis_index("seq")
-    incoming = incoming.reshape(slots, steps, -1)
     appended = jnp.where(owned_here[..., None], incoming, jnp.zeros((), jnp.bfloat16))
-    return (outputs, appended[:, None])
+    return (outputs.astype(jnp.bfloat16), appended[:, None])
 
 
 def body(

time: 78.3 us -> 70.6 us (0.902)
  local copies, waits for them, and re-layouts: 6.74 us -> 0.18 us
  Pallas kernels: 68.2 us -> 64.6 us
  other arithmetic: 2.37 us -> 4.96 us
    pallas_call x1, Pallas kernels: 68.2 us -> 64.6 us  [run_layer(): pl.pallas_call(functools.partial(layer_kernel, ring, plane, steps), out_s...]
    reshape x3 -> x0, local copies, waits for them, and re-layouts: 3.58 us -> none  [the longest x1 1.31 us: whole_layer(): mlp_gain.reshape(1, -1)]
    unnamed x4 -> x2, local copies, waits for them, and re-layouts: 2.98 us -> 0.01 us
    convert_element_type x0 -> x1, other arithmetic: none -> 1.7 us  [whole_layer(): return (outputs.astype(jnp.bfloat16), appended[:, None])]
    unnamed x0 -> x1, other arithmetic: none -> 1.68 us
where the time goes in v3:
time: 70.6 us; the launch traced here: 70.4 us
  Pallas kernels  64.6 us (92%)
  other arithmetic  4.96 us (7%)
    pallas_call x1, Pallas kernels, run_layer(): pl.pallas_call(functools.partial(layer_kernel, ring, plane, steps), out_s...  64.6 us
    convert_element_type x1, other arithmetic, whole_layer(): return (outputs.astype(jnp.bfloat16), appended[:, None])  1.7 us
    unnamed x1, other arithmetic  1.68 us

profile of v3, /device:TPU:0, one launch (start us, length us, event | category | flops | bytes accessed | tf_op | source)
XLA Modules:
  0.0 70.4 jit_solution(6812474116466782501)
XLA Ops:
  0.6 0.7 %add_convert_fusion = f32[8,4]{1,0:T(8,128)S(1)} fusion(s32[8]{0:T(128)} %length_ref.1), kind=kLoop, calls=%fused_computation.6 | loop fusion | flops 64 | bytes 160 | tf_op jit(solution)/shard_map/convert_element_type | solution.py:467
  1.4 0.1 convert_element_type.14
  1.4 0.1 fusion
  1.6 0.7 pad_maximum_fusion
  2.3 0.0 copy-start
  2.3 64.6 %shard_map.176 = (f32[8,4,2560]{2,1,0:T(4,128)}, bf16[8,4,2048]{2,1,0:T(4,128)(2,1)}) custom-call(s32[32]{0:T(128)} %slot_ref.1, s32[8]{0:T(128)} %length_ref.1, s32[4,8]{1,0:T(4,128)} %bitcast.15, bf16[8,4,2560]{2,1,0:T(4,128)(2,1)} %tokens_ref.1, f32[20,128]{1,0:T(8,128)} %bitcast.13, f32[1,128]{1,0:T(1,128)} %bitcast.16, f32[1,128]{1,0:T(1,128)} %bitcast.17, ...), custom_call_target="tpu_custom_call" | custom-call | tf_op jit(solution)/shard_map/pallas_call | solution.py:406
  66.9 1.7 %convert_element_type.15 = bf16[8,4,2560]{2,1,0:T(4,128)(2,1)} convert(f32[8,4,2560]{2,1,0:T(4,128)} %get-tuple-element.4) | non-fusion elementwise | flops 81920 | bytes 491520 | tf_op jit(solution)/shard_map/convert_element_type | solution.py:490
  68.6 0.0 copy-done
  68.6 0.1 copy.21
  68.7 1.7 %select_bitcast_fusion = bf16[8,1,4,2048]{3,2,1,0:T(4,128)(2,1)} fusion(bf16[8,4,2048]{2,1,0:T(4,128)(2,1)} %get-tuple-element.5, pred[8,4]{1,0:T(8,128)(4,1)S(1)} %copy.21), kind=kLoop, calls=%fused_computation | loop fusion | flops 65536 | bytes 262176
  (2 shorter events, 0.0 us)
Async XLA Ops:
  2.3 66.3 %copy-start = (s32[8,4]{0,1:T(4,128)S(1)}, s32[8,4]{0,1:T(4,128)}, u32[]{:S(2)}) copy-start(s32[8,4]{0,1:T(4,128)} %param.20) | copy-start | bytes 388

commit v4 on v3

--- a/solution.py
+++ b/solution.py
@@ -382,7 +382,7 @@
     copies = [send(own, own, (group, peer)) for peer in plane_peers]
     for copy in copies:
         copy.wait_recv()
-    out_ref[...] = final[...].astype(f32)
+    out_ref[...] = final[...]
     for copy in sent:
         copy.wait_send()
 
@@ -406,7 +406,7 @@
     return pl.pallas_call(
         functools.partial(layer_kernel, ring, plane, steps),
         out_shape=(
-            jax.ShapeDtypeStruct((plane, steps, width), f32),
+            jax.ShapeDtypeStruct((plane, steps, width), bf16),
             jax.ShapeDtypeStruct((slots, steps, 2 * plane * head_dim), bf16),
         ),
         in_specs=[smem] * len(scalars) + [vmem] * len(vectors) + [anywhere] * len(matrices),
@@ -439,6 +439,33 @@
         ],
         compiler_params=pltpu.CompilerParams(collective_id=0, has_side_effects=True),
     )(*scalars, *vectors, *matrices)
+
+
+def finish_kernel(shard_ref, owner_ref, final_ref, incoming_ref, out_ref, appended_ref):
+    slots, steps, width = incoming_ref.shape
+    out_ref[...] = final_ref[...]
+    row = lax.broadcasted_iota(jnp.int32, (steps, width), 0)
+    for j in range(slots):
+        owned = row < 0
+        for t in range(steps):
+            owned = owned | (row == jnp.where(owner_ref[t, j] == shard_ref[0], t, -1))
+        kept = jnp.where(owned, incoming_ref[j].astype(jnp.float32), 0.0)
+        appended_ref[j, 0] = kept.astype(appended_ref.dtype)
+
+
+def run_finish(shard, owner, final, incoming):
+    slots, steps, width = incoming.shape
+    vmem = pl.BlockSpec(memory_space=pltpu.VMEM)
+    smem = pl.BlockSpec(memory_space=pltpu.SMEM)
+    return pl.pallas_call(
+        finish_kernel,
+        out_shape=(
+            jax.ShapeDtypeStruct(final.shape, final.dtype),
+            jax.ShapeDtypeStruct((slots, 1, steps, width), incoming.dtype),
+        ),
+        in_specs=[smem, smem, vmem, vmem],
+        out_specs=(vmem, vmem),
+    )(shard, owner, final, incoming)
 
 
 def whole_layer(
@@ -485,9 +512,8 @@
         ),
         ring, plane, steps,
     )
-    owned_here = owner_shard == lax.axis_index("seq")
-    appended = jnp.where(owned_here[..., None], incoming, jnp.zeros((), jnp.bfloat16))
-    return (outputs.astype(jnp.bfloat16), appended[:, None])
+    shard = lax.axis_index("seq").astype(jnp.int32).reshape(1)
+    return run_finish(shard, owner_shard.T, outputs, incoming)
 
 
 def body(

time: 70.6 us -> 68.7 us (0.973)
  other arithmetic: 4.96 us -> 1.58 us
  Pallas kernels: 64.6 us -> 66.2 us
    pallas_call x0 -> x1, Pallas kernels: none -> 1.74 us  [run_finish(): pl.pallas_call(finish_kernel, out_shape=(jax.ShapeDtypeStruct(final.shape...]
    convert_element_type x1 -> x0, other arithmetic: 1.7 us -> none  [whole_layer(): return (outputs.astype(jnp.bfloat16), appended[:, None])]
    unnamed x1 -> x0, other arithmetic: 1.68 us -> none
where the time goes in v4:
time: 68.7 us; the launch traced here: 68.5 us
  Pallas kernels  66.2 us (96%)
  other arithmetic  1.58 us (2%)
    pallas_call x1, Pallas kernels, run_layer(): pl.pallas_call(functools.partial(layer_kernel, ring, plane, steps), out_s...  64.5 us
    pallas_call x1, Pallas kernels, run_finish(): pl.pallas_call(finish_kernel, out_shape=(jax.ShapeDtypeStruct(final.shape...  1.74 us

profile of v4, /device:TPU:0, one launch (start us, length us, event | category | flops | bytes accessed | tf_op | source)
XLA Modules:
  0.0 68.5 jit_solution(13321614034361196812)
XLA Ops:
  0.6 0.7 %add_convert_fusion = f32[8,4]{1,0:T(8,128)S(1)} fusion(s32[8]{0:T(128)} %length_ref.1), kind=kLoop, calls=%fused_computation.5 | loop fusion | flops 64 | bytes 160 | tf_op jit(solution)/shard_map/convert_element_type | solution.py:494
  1.4 0.1 convert_element_type.11
  1.5 0.1 fusion
  1.6 0.7 %pad_maximum_fusion = (f32[32,128]{1,0:T(8,128)}, f32[32,128]{1,0:T(8,128)}) fusion(f32[32,64]{1,0:T(8,128)S(1)} %get-tuple-element.8, f32[32,64]{1,0:T(8,128)S(1)} %get-tuple-element.7, f32[32,64]{1,0:T(8,128)S(1)} %get-tuple-element.6), kind=kLoop, calls=%fused_computation.2 | loop fusion | flops 8192 | bytes 57344 | tf_op jit(solution)/shard_map/concatenate | solution.py:505
  2.3 64.5 %shard_map.176 = (bf16[8,4,2560]{2,1,0:T(4,128)(2,1)}, bf16[8,4,2048]{2,1,0:T(4,128)(2,1)}) custom-call(s32[32]{0:T(128)} %slot_ref.1, s32[8]{0:T(128)} %length_ref.1, s32[4,8]{1,0:T(4,128)} %bitcast.12, bf16[8,4,2560]{2,1,0:T(4,128)(2,1)} %tokens_ref.1, f32[20,128]{1,0:T(8,128)} %bitcast.10, f32[1,128]{1,0:T(1,128)} %bitcast.14, f32[1,128]{1,0:T(1,128)} %bitcast.15, ...), custom_call_target="tpu_custom_call" | custom-call | tf_op jit(solution)/shard_map/pallas_call | solution.py:406
  66.8 1.7 %shard_map.177 = (bf16[8,4,2560]{2,1,0:T(4,128)(2,1)}, bf16[8,1,4,2048]{3,2,1,0:T(4,128)(2,1)}) custom-call(s32[1]{0:T(128)} %bitcast.shard_ref, s32[4,8]{1,0:T(4,128)} %bitcast.13, bf16[8,4,2560]{2,1,0:T(4,128)(2,1)} %get-tuple-element.4.final_ref, bf16[8,4,2048]{2,1,0:T(4,128)(2,1)} %get-tuple-element.5.incoming_ref), custom_call_target="tpu_custom_call" | custom-call | tf_op jit(solution)/shard_map/pallas_call | solution.py:460
  (1 shorter events, 0.0 us)
